TPU v7x, 32 devices: a whole 2x2x4 slice. The times are simulated.
32 devices in a mesh: bucket: 4 (over y, core), dp: 8 (over z, x).
Axes of the slice: x: 2, y: 2, z: 4, core: 2. Of those that a mesh axis runs over, the one named last changes fastest.
Arguments:
- tokens: bfloat16 [32768, 768], P(('bucket', 'dp')), may hold values from -6 to 6
- segment: int32 [32768], P(('bucket', 'dp')), may hold values from 0 to 1023, as said below
- live: int32 [32768], P(('bucket', 'dp')), may hold values from 0 to 1, as said below
- group_patches: int32 [4], replicated, may hold values from 8192 to 65535
- qkv_weight: bfloat16 [768, 2304], replicated, may hold values from -0.21875 to 0.21875
- qkv_bias: float32 [2304], replicated, may hold values from -4 to 4
- out_weight: bfloat16 [768, 768], replicated, may hold values from -0.625 to 0.625
- out_bias: float32 [768], replicated, may hold values from -4 to 4
- fc1_weight: bfloat16 [768, 3072], replicated, may hold values from -0.21875 to 0.21875
- fc1_bias: float32 [3072], replicated, may hold values from -4 to 4
- fc2_weight: bfloat16 [3072, 768], replicated, may hold values from -0.109375 to 0.109375
- fc2_bias: float32 [768], replicated, may hold values from -4 to 4
- norm_gain: float32 [2, 768], replicated, may hold values from 0.1 to 1.9
- norm_shift: float32 [2, 768], replicated, may hold values from -4 to 4
- qk_gain: float32 [2, 64], replicated, may hold values from 0.1 to 1.9
- qk_shift: float32 [2, 64], replicated, may hold values from -4 to 4
- cotangent: bfloat16 [32768, 768], P(('bucket', 'dp')), may hold values from -6 to 6
Outputs:
- out: bfloat16 [32768, 768], P(('bucket', 'dp'))
- tokens_grad: float32 [32768, 768], P(('bucket', 'dp'))
- qkv_weight_grad: float32 [768, 2304], replicated
- qkv_bias_grad: float32 [2304], replicated
- out_weight_grad: float32 [768, 768], replicated
- out_bias_grad: float32 [768], replicated
- fc1_weight_grad: float32 [768, 3072], replicated
- fc1_bias_grad: float32 [3072], replicated
- fc2_weight_grad: float32 [3072, 768], replicated
- fc2_bias_grad: float32 [768], replicated
- norm_gain_grad: float32 [2, 768], replicated
- norm_shift_grad: float32 [2, 768], replicated
- qk_gain_grad: float32 [2, 64], replicated
- qk_shift_grad: float32 [2, 64], replicated
Inputs may be any that keep to these rules, and one draw needn't show every extreme that they name: Each row's id is the index, within its device's 1024 rows, of the first row of its segment, so along a device the ids never fall and the first is 0. The rows hold whole sequences of 256 rows on devices in the first half of the bucket axis and of 1024 rows on the others; no segment spans two sequences. The rows with live 0 lie at the tail of their sequence, at most a quarter of it, and form one segment of their own; the last sequence of each device ends with exactly one such row. `live`: 0 only on the tail padding of a sequence.
All inputs are finite; a program needn't handle non-finite values.
Results may differ from a plain program's by a relative error of at most 0.013.
Values sent between devices are 32-bit elements; how exact they have to be, the bound alone decides.
A program may use at most 256 MiB of HBM per device.

v0:
```python
import math

import jax
import jax.numpy as jnp
from jax import lax
from jax.sharding import PartitionSpec as P

HEADS = 12
HD = 64
LONG = 1024


EPSILON = 1e-06
MASKED = -1e30


def norm_forward(values, gains, shifts):
    center = values - jnp.mean(values, axis=-1, keepdims=True)
    inverse = lax.rsqrt(jnp.mean(center * center, axis=-1, keepdims=True) + EPSILON)
    unit_vals = center * inverse
    return (unit_vals * gains + shifts, unit_vals, inverse)


def norm_backward(grads, unit_vals, inverse, gains):
    scaled = grads * gains
    inner = (
        scaled
        - jnp.mean(scaled, axis=-1, keepdims=True)
        - unit_vals * jnp.mean(scaled * unit_vals, axis=-1, keepdims=True)
    )
    return inverse * inner


def attend_forward(query_rows, query_segs, key_rows, value_rows, key_segs):
    scores = jnp.einsum("ihd,jhd->hij", query_rows, key_rows, preferred_element_type=jnp.float32)
    same_seg = query_segs[:, None] == key_segs[None, :]
    scores = jnp.where(same_seg[None], scores, MASKED)
    row_max = jnp.max(scores, axis=-1, keepdims=True)
    log_total = row_max + jnp.log(jnp.sum(jnp.exp(scores - row_max), axis=-1, keepdims=True))
    probs_low = jnp.exp(scores - log_total).astype(jnp.bfloat16)
    attention = jnp.einsum(
        "hij,jhd->ihd", probs_low, value_rows, preferred_element_type=jnp.float32
    )
    return (attention, log_total)


def attend_backward(query_rows, query_segs, key_rows, value_rows, key_segs, log_total, out_grad):
    scores = jnp.einsum("ihd,jhd->hij", query_rows, key_rows, preferred_element_type=jnp.float32)
    same_seg = query_segs[:, None] == key_segs[None, :]
    probs = jnp.where(same_seg[None], jnp.exp(scores - log_total), 0.0)
    probs_low = probs.astype(jnp.bfloat16)
    value_part = jnp.einsum("hij,ihd->jhd", probs_low, out_grad, preferred_element_type=jnp.float32)
    prob_grad = jnp.einsum("ihd,jhd->hij", out_grad, value_rows, preferred_element_type=jnp.float32)
    delta_sum = jnp.sum(probs * prob_grad, axis=-1, keepdims=True)
    score_low = (probs * (prob_grad - delta_sum)).astype(jnp.bfloat16)
    query_part = jnp.einsum("hij,jhd->ihd", score_low, key_rows, preferred_element_type=jnp.float32)
    key_part = jnp.einsum("hij,ihd->jhd", score_low, query_rows, preferred_element_type=jnp.float32)
    return (query_part, key_part, value_part)


def add_rows(total, part):
    return total + part


def body(
    tokens,
    segment,
    live,
    group_patches,
    qkv_weight,
    qkv_bias,
    out_weight,
    out_bias,
    fc1_weight,
    fc1_bias,
    fc2_weight,
    fc2_bias,
    norm_gain,
    norm_shift,
    qk_gain,
    qk_shift,
    cotangent,
):
    row_count, features = tokens.shape
    query_block = min(512, LONG)
    block_count = row_count // query_block
    root_head = math.sqrt(HD)
    inputs = tokens.astype(jnp.float32)
    a_val, a_unit, a_inverse = norm_forward(inputs, norm_gain[0], norm_shift[0])
    a_low = a_val.astype(jnp.bfloat16)
    qkv = jnp.dot(a_low, qkv_weight, preferred_element_type=jnp.float32) + qkv_bias
    query_raw = qkv[:, :features].reshape(row_count, HEADS, HD)
    key_raw = qkv[:, features : 2 * features].reshape(row_count, HEADS, HD)
    value_raw = qkv[:, 2 * features :].reshape(row_count, HEADS, HD)
    query_norm, query_unit, query_inverse = norm_forward(query_raw, qk_gain[0], qk_shift[0])
    key_norm, key_unit, key_inverse = norm_forward(key_raw, qk_gain[1], qk_shift[1])
    query_low = (query_norm / root_head).astype(jnp.bfloat16)
    key_low = key_norm.astype(jnp.bfloat16)
    value_low = value_raw.astype(jnp.bfloat16)

    def forward_block(number):
        begin_row = number * query_block
        query_rows = lax.dynamic_slice_in_dim(query_low, begin_row, query_block, 0)
        query_segs = lax.dynamic_slice_in_dim(segment, begin_row, query_block, 0)
        return attend_forward(query_rows, query_segs, key_low, value_low, segment)

    attn_blocks, total_blocks = lax.map(forward_block, jnp.arange(block_count, dtype=jnp.int32))
    attn_low = attn_blocks.reshape(row_count, features).astype(jnp.bfloat16)
    hidden = inputs + jnp.dot(attn_low, out_weight, preferred_element_type=jnp.float32) + out_bias
    c_val, c_unit, c_inverse = norm_forward(hidden, norm_gain[1], norm_shift[1])
    c_low = c_val.astype(jnp.bfloat16)
    preact = jnp.dot(c_low, fc1_weight, preferred_element_type=jnp.float32) + fc1_bias
    g_low = jax.nn.gelu(preact, approximate=False).astype(jnp.bfloat16)
    mlp_out = jnp.dot(g_low, fc2_weight, preferred_element_type=jnp.float32) + fc2_bias
    live_rows = live.astype(jnp.float32)[:, None]
    out = (live_rows * (hidden + mlp_out)).astype(jnp.bfloat16)
    mlp_grad = cotangent.astype(jnp.float32) * live_rows
    mlp_low = mlp_grad.astype(jnp.bfloat16)
    fc2_w_term = jnp.einsum("tf,td->fd", g_low, mlp_low, preferred_element_type=jnp.float32)
    fc2_b_term = jnp.sum(mlp_grad, axis=0)
    gelu_grad = jnp.einsum("td,fd->tf", mlp_low, fc2_weight, preferred_element_type=jnp.float32)
    slope = 0.5 * (1.0 + jax.scipy.special.erf(preact / math.sqrt(2.0))) + preact * jnp.exp(
        -0.5 * preact * preact
    ) / math.sqrt(2.0 * math.pi)
    pre_low = (gelu_grad * slope).astype(jnp.bfloat16)
    fc1_w_term = jnp.einsum("td,tf->df", c_low, pre_low, preferred_element_type=jnp.float32)
    fc1_b_term = jnp.sum(pre_low.astype(jnp.float32), axis=0)
    norm_in_grad = jnp.einsum("tf,df->td", pre_low, fc1_weight, preferred_element_type=jnp.float32)
    gain_second = jnp.sum(norm_in_grad * c_unit, axis=0)
    shift_second = jnp.sum(norm_in_grad, axis=0)
    hidden_grad = mlp_grad + norm_backward(norm_in_grad, c_unit, c_inverse, norm_gain[1])
    branch_low = hidden_grad.astype(jnp.bfloat16)
    out_w_term = jnp.einsum("td,te->de", attn_low, branch_low, preferred_element_type=jnp.float32)
    out_b_term = jnp.sum(branch_low.astype(jnp.float32), axis=0)
    attn_grad_low = jnp.einsum(
        "te,de->td", branch_low, out_weight, preferred_element_type=jnp.float32
    ).astype(jnp.bfloat16)
    attn_grad_heads = attn_grad_low.reshape(row_count, HEADS, HD)

    def backward_block(sums, item):
        number, log_total = item
        begin_row = number * query_block
        query_rows = lax.dynamic_slice_in_dim(query_low, begin_row, query_block, 0)
        query_segs = lax.dynamic_slice_in_dim(segment, begin_row, query_block, 0)
        out_grad = lax.dynamic_slice_in_dim(attn_grad_heads, begin_row, query_block, 0)
        query_part, key_part, value_part = attend_backward(
            query_rows, query_segs, key_low, value_low, segment, log_total, out_grad
        )
        return ((add_rows(sums[0], key_part), add_rows(sums[1], value_part)), query_part)

    empty_heads = jnp.zeros((row_count, HEADS, HD), jnp.float32)
    (key_grad, value_grad), query_blocks = lax.scan(
        backward_block,
        (empty_heads, empty_heads),
        (jnp.arange(block_count, dtype=jnp.int32), total_blocks),
    )
    query_grad = query_blocks.reshape(row_count, HEADS, HD) / root_head
    qgain_term = jnp.sum(query_grad * query_unit, axis=(0, 1))
    kgain_term = jnp.sum(key_grad * key_unit, axis=(0, 1))
    qshift_term = jnp.sum(query_grad, axis=(0, 1))
    kshift_term = jnp.sum(key_grad, axis=(0, 1))
    query_in = norm_backward(query_grad, query_unit, query_inverse, qk_gain[0]).reshape(
        row_count, features
    )
    key_in = norm_backward(key_grad, key_unit, key_inverse, qk_gain[1]).reshape(row_count, features)
    qkv_grad_low = jnp.concatenate(
        [query_in, key_in, value_grad.reshape(row_count, features)], axis=1
    ).astype(jnp.bfloat16)
    qkv_w_term = jnp.einsum("td,te->de", a_low, qkv_grad_low, preferred_element_type=jnp.float32)
    qkv_b_term = jnp.sum(qkv_grad_low.astype(jnp.float32), axis=0)
    first_grad = jnp.einsum(
        "te,de->td", qkv_grad_low, qkv_weight, preferred_element_type=jnp.float32
    )
    gain_first = jnp.sum(first_grad * a_unit, axis=0)
    shift_first = jnp.sum(first_grad, axis=0)
    tokens_grad = hidden_grad + norm_backward(first_grad, a_unit, a_inverse, norm_gain[0])
    small_terms = jnp.concatenate(
        [
            qkv_b_term,
            out_b_term,
            fc1_b_term,
            fc2_b_term,
            gain_first,
            gain_second,
            shift_first,
            shift_second,
            qgain_term,
            kgain_term,
            qshift_term,
            kshift_term,
        ]
    )
    counts = group_patches.astype(jnp.float32)
    own_count = jnp.sum(
        jnp.where(jnp.arange(counts.shape[0]) == lax.axis_index("bucket"), counts, 0.0)
    )
    weighting = own_count / (jnp.sum(counts) * math.sqrt(row_count * lax.axis_size("dp")))
    flat_terms = (
        qkv_w_term.reshape(-1),
        out_w_term.reshape(-1),
        fc1_w_term.reshape(-1),
        fc2_w_term.reshape(-1),
        small_terms,
    )
    shares = (
        lax.psum_scatter(flat_terms[0], "dp", scatter_dimension=0, tiled=True),
        lax.psum_scatter(flat_terms[1], "dp", scatter_dimension=0, tiled=True),
        lax.psum_scatter(flat_terms[2], "dp", scatter_dimension=0, tiled=True),
        lax.psum_scatter(flat_terms[3], "dp", scatter_dimension=0, tiled=True),
        lax.psum_scatter(flat_terms[4], "dp", scatter_dimension=0, tiled=True),
    )
    merged = lax.psum(
        (
            weighting * shares[0],
            weighting * shares[1],
            weighting * shares[2],
            weighting * shares[3],
            weighting * shares[4],
        ),
        "bucket",
    )
    finished = (
        lax.all_gather(merged[0], "dp", axis=0, tiled=True),
        lax.all_gather(merged[1], "dp", axis=0, tiled=True),
        lax.all_gather(merged[2], "dp", axis=0, tiled=True),
        lax.all_gather(merged[3], "dp", axis=0, tiled=True),
        lax.all_gather(merged[4], "dp", axis=0, tiled=True),
    )
    hidden_units = fc1_weight.shape[1]
    small_done = finished[4]
    offset_one = 3 * features
    offset_two = offset_one + features
    offset_three = offset_two + hidden_units
    offset_four = offset_three + features
    offset_five = offset_four + 2 * features
    offset_six = offset_five + 2 * features
    offset_seven = offset_six + 2 * HD
    return (
        out,
        tokens_grad,
        finished[0].reshape(features, 3 * features),
        small_done[:offset_one],
        finished[1].reshape(features, features),
        small_done[offset_one:offset_two],
        finished[2].reshape(features, hidden_units),
        small_done[offset_two:offset_three],
        finished[3].reshape(hidden_units, features),
        small_done[offset_three:offset_four],
        small_done[offset_four:offset_five].reshape(2, features),
        small_done[offset_five:offset_six].reshape(2, features),
        small_done[offset_six:offset_seven].reshape(2, HD),
        small_done[offset_seven:].reshape(2, HD),
    )


def solution(mesh):
    return jax.shard_map(
        body,
        mesh=mesh,
        in_specs=(
            P(("bucket", "dp"), None),
            P(("bucket", "dp")),
            P(("bucket", "dp")),
            P(),
            P(),
            P(),
            P(),
            P(),
            P(),
            P(),
            P(),
            P(),
            P(),
            P(),
            P(),
            P(),
            P(("bucket", "dp"), None),
        ),
        out_specs=(
            P(("bucket", "dp"), None),
            P(("bucket", "dp"), None),
            P(),
            P(),
            P(),
            P(),
            P(),
            P(),
            P(),
            P(),
            P(),
            P(),
            P(),
            P(),
        ),
        check_vma=False,
    )
```

profile of v0, /device:TPU:0, one launch (start us, length us, event | category | flops | bytes accessed | tf_op | source)
XLA Modules:
  0.0 1998.4 jit_solution(12137669085669119188)
XLA Ops:
  67.8 78.4 %while.27 = (s32[]{:T(128)}, bf16[2,512,12,64]{1,3,2,0:T(8,128)(2,1)}, f32[2,12,512,1]{2,1,3,0:T(8,128)}, s32[2]{0:T(128)S(1)}, s32[1024]{0:T(1024)S(1)}, /*inde...) while((s32[]{:T(128)}, ...), condition=%wide.region_9.10_spmd, body=%wide.region_6.9_spmd.sunk | while | flops 1661462528 | bytes 102615376 | solution.py:107
  69.7 13.6 select_reduce_fusion.2
  83.4 11.6 exponential_reduce_fusion.2
  108.8 13.6 select_reduce_fusion.2
  122.5 11.6 exponential_reduce_fusion.2
  156.8 48.4 %fusion.27 = (bf16[1024,3072]{1,0:T(8,128)(2,1)}, f32[1024,3072]{1,0:T(8,128)S(1)}) fusion(f32[3072]{0:T(1024)} %param.30, bf16[768,3072]{1,0:T(8,128)(2,1)} %param.29, f32[1024,768]{0,1:T(8,128)} %copy-done.13, f32[768]{0:T(1024)} %get-tuple-element.234, f32[768]{0:T(1024)S(1)} %copy-done.50, f32[1024]{0:T(1024)S(1)} %add_rsqrt_fusion.2, ...), kind=kOutput, calls=%fused_computation.41 | convolution fusion | flops 5043388416 | bytes 26765312 | tf_op jit(solution)/shard_map/dot_general | solution.py:112
  216.5 11.9 fusion.76
  253.8 243.2 %while.28 = (s32[]{:T(128)}, f32[1024,12,64]{0,2,1:T(8,128)}, f32[1024,12,64]{0,2,1:T(8,128)}, f32[2,512,12,64]{1,0,3,2:T(2,128)}, s32[2]{0:T(128)S(1)}, /*index...) while((s32[]{:T(128)}, f32[1024,12,64]{0,2,1:T(8,128)}, ...), condition=%wide.region_16.17_spmd.clone, body=%wide.region_14.16_spmd.clone.sunk | while | flops 4105693184 | bytes 253200816 | solution.py:152
  255.2 13.4 fusion.121
  270.5 18.0 multiply_reduce_fusion.16
  288.5 22.1 %multiply_convert_fusion.6 = bf16[12,512,1024]{2,1,0:T(8,128)(2,1)} fusion(f32[12,512,1024]{2,1,0:T(8,128)} %get-tuple-element.445, f32[12,512,1024]{2,1,0:T(8,128)} %fusion.121, f32[12,512]{1,0:T(8,128)} %get-tuple-element.446, f32[12,512]{1,0:T(8,128)} %dynamic-slice_bitcast_fusion.2, pred[512,1024]{1,0:T(8,128)(4,1)} %broadcast_compare_fusion.5), kind=kLoop, calls=%fused_computation.13.clone.1 | loop fusion | flops 31457280 | bytes 63488000 | tf_op jit(solution)/shard_map/while/body/eval_jaxpr/convert_element_type | solution.py:55
  346.0 28.8 %dynamic_update_slice.19 = f32[2,512,12,64]{1,0,3,2:T(2,128)} dynamic-update-slice(f32[2,512,12,64]{1,0,3,2:T(2,128)} %get-tuple-element.501, f32[1,512,12,64]{1,0,3,2:T(1,128)} %copy.139, s32[]{:T(128)S(6)} %copy.156, s32[]{:T(128)} %constant.67.clone.1..sunk.1, s32[]{:T(128)} %constant.67.clone.1..sunk.1, s32[]{:T(128)} %constant.67.clone.1..sunk.1) | dynamic-update-slice | bytes 3145732 | tf_op jit(solution)/shard_map/while/body/jit(dynamic_update_index_in_dim)/dynamic_update_slice | solution.py:107
  376.1 13.4 fusion.121
  391.4 18.0 multiply_reduce_fusion.16
  409.4 22.1 %multiply_convert_fusion.6 = bf16[12,512,1024]{2,1,0:T(8,128)(2,1)} fusion(f32[12,512,1024]{2,1,0:T(8,128)} %get-tuple-element.445, f32[12,512,1024]{2,1,0:T(8,128)} %fusion.121, f32[12,512]{1,0:T(8,128)} %get-tuple-element.446, f32[12,512]{1,0:T(8,128)} %dynamic-slice_bitcast_fusion.2, pred[512,1024]{1,0:T(8,128)(4,1)} %broadcast_compare_fusion.5), kind=kLoop, calls=%fused_computation.13.clone.1 | loop fusion | flops 31457280 | bytes 63488000 | tf_op jit(solution)/shard_map/while/body/eval_jaxpr/convert_element_type | solution.py:55
  467.8 28.8 %dynamic_update_slice.19 = f32[2,512,12,64]{1,0,3,2:T(2,128)} dynamic-update-slice(f32[2,512,12,64]{1,0,3,2:T(2,128)} %get-tuple-element.501, f32[1,512,12,64]{1,0,3,2:T(1,128)} %copy.139, s32[]{:T(128)S(6)} %copy.156, s32[]{:T(128)} %constant.67.clone.1..sunk.1, s32[]{:T(128)} %constant.67.clone.1..sunk.1, s32[]{:T(128)} %constant.67.clone.1..sunk.1) | dynamic-update-slice | bytes 3145732 | tf_op jit(solution)/shard_map/while/body/jit(dynamic_update_index_in_dim)/dynamic_update_slice | solution.py:107
  619.6 834.4 %all-reduce.10.cloned.1.call-done = (f32[1769472]{0:T(1024)}, f32[589824]{0:T(1024)}, f32[2359296]{0:T(1024)}, f32[2359296]{0:T(1024)}) async-done(((f32[1769472]{0:T(1024)}, f32[589824]{0:T(1024)}, f32[2359296]{0:T(1024)}, f32[2359296]{0:T(1024)}), (f32[1769472]{0:T(1024)}, f32[589824]{0:T(1024)}, f32[2359296]{0:T(1024)}, f32[2359296]{0:T(1024)})) %all-reduce.10.cloned.1.call-update) | async-done | bytes 28311568
  1462.6 74.4 %all-reduce.12.cloned.1.call-done = (f32[221184]{0:T(1024)}, f32[73728]{0:T(1024)}, f32[294912]{0:T(1024)}, f32[294912]{0:T(1024)}) async-done(((f32[221184]{0:T(1024)}, f32[73728]{0:T(1024)}, f32[294912]{0:T(1024)}, f32[294912]{0:T(1024)}), (f32[221184]{0:T(1024)}, f32[73728]{0:T(1024)}, f32[294912]{0:T(1024)}, f32[294912]{0:T(1024)})) %all-reduce.12.cloned.1.call-update) | async-done | bytes 3538960 | tf_op jit(solution)/shard_map/psum | solution.py:212
  1558.8 39.3 %all-reduce.1 = f32[10240]{0:T(1024)} all-reduce(f32[10240]{0:T(1024)} %concatenate.8), channel_id=3, replica_groups=mesh['bucket'=4,'dp'=8] {'dp'}, use_global_device_ids=true, to_apply=%region_39.40.clone | all-reduce | flops 10240 | bytes 81920
  1606.2 31.1 %all-gather = f32[8,1,1280]{2,1,0:T(1,128)S(1)} all-gather(f32[1,1,1280]{2,1,0:T(1,128)S(1)} %reshape.338), channel_id=1, replica_groups=mesh['bucket'=4,'dp'=8] {'dp'}, dimensions={0}, use_global_device_ids=true | all-gather | bytes 46080 | tf_op jit(solution)/shard_map/all_gather | solution.py:227
  1671.0 32.0 %all-gather.6.cloned.1.call-done = f32[1769472]{0:T(1024)} async-done(((f32[221184]{0:T(1024)}), f32[1769472]{0:T(1024)}) %all-gather.6.cloned.1.call-update) | async-done | bytes 7077904 | tf_op jit(solution)/shard_map/all_gather | solution.py:223
  1711.2 130.3 %all-gather.10.cloned.1.call-done = f32[2359296]{0:T(1024)} async-done(((f32[294912]{0:T(1024)}), f32[2359296]{0:T(1024)}) %all-gather.10.cloned.1.call-update) | async-done | bytes 9437200 | tf_op jit(solution)/shard_map/all_gather | solution.py:225
  1852.6 127.5 %all-gather.12.cloned.1.call-done = f32[2359296]{0:T(1024)} async-done(((f32[294912]{0:T(1024)}), f32[2359296]{0:T(1024)}) %all-gather.12.cloned.1.call-update) | async-done | bytes 9437200 | tf_op jit(solution)/shard_map/all_gather | solution.py:226
  1980.1 11.3 reshape.333
  (328 shorter events, 419.9 us)
Async XLA Ops:
  7.2 1446.8 %all-reduce.10.cloned.1.call-start = ((), (), s32[]{:S(2)}) async-start(), calls=%async_computation.4 | async-start | bytes 56623104
  45.5 20.4 %copy-start.55 = (f32[64]{0:T(128)}, f32[64]{0:T(128)S(1)}, u32[]{:S(2)}) copy-start(f32[64]{0:T(128)S(1)} %get-tuple-element.318) | copy-start | bytes 772
  83.4 11.7 copy-start.36
  83.4 11.7 copy-start.7
  83.4 11.7 copy-start.29
  95.1 10.9 copy-start.37
  122.5 11.7 copy-start.36
  122.5 11.7 copy-start.7
  122.5 11.7 copy-start.29
  134.1 10.9 copy-start.37
  156.8 48.5 %copy-start.22 = (bf16[1024,768]{0,1:T(8,128)(2,1)S(1)}, bf16[1024,768]{0,1:T(8,128)(2,1)}, u32[]{:S(2)}) copy-start(bf16[1024,768]{0,1:T(8,128)(2,1)} %copy.81) | copy-start | bytes 4718596
  156.8 48.5 %copy-start.51 = (f32[1024]{0:T(1024)S(1)}, f32[1024]{0:T(1024)}, u32[]{:S(2)}) copy-start(f32[1024]{0:T(1024)} %convert_element_type.71) | copy-start | bytes 12292
  156.8 48.5 %copy-start.69 = (f32[3072]{0:T(1024)S(1)}, f32[3072]{0:T(1024)}, u32[]{:S(2)}) copy-start(f32[3072]{0:T(1024)} %param.30) | copy-start | bytes 36868
  216.5 11.9 copy-start.72
  255.2 13.4 copy-start.38
  376.1 13.5 copy-start.38
  431.5 10.0 copy-start.5
  431.5 10.0 copy-start.12
  431.5 10.0 copy-start.17
  614.5 922.6 %all-reduce.12.cloned.1.call-start = ((), (), s32[]{:S(2)}) async-start(), calls=%async_computation.5 | async-start | bytes 7077888 | tf_op jit(solution)/shard_map/psum | solution.py:212
  1462.6 205.1 %all-gather.8.cloned.1.call-start = ((), (), s32[]{:S(2)}) async-start(), calls=%async_computation.1 | async-start | bytes 2654208 | tf_op jit(solution)/shard_map/all_gather | solution.py:224
  1537.1 165.9 %all-gather.6.cloned.1.call-start = ((), (), s32[]{:S(2)}) async-start(), calls=%async_computation | async-start | bytes 7962624 | tf_op jit(solution)/shard_map/all_gather | solution.py:223
  1537.7 303.9 %all-gather.10.cloned.1.call-start = ((), (), s32[]{:S(2)}) async-start(), calls=%async_computation.2 | async-start | bytes 10616832 | tf_op jit(solution)/shard_map/all_gather | solution.py:225
  1538.2 441.8 %all-gather.12.cloned.1.call-start = ((), (), s32[]{:S(2)}) async-start(), calls=%async_computation.3 | async-start | bytes 10616832 | tf_op jit(solution)/shard_map/all_gather | solution.py:226
  (68 other events, 312.2 us)
Sparse Core Ops, SparseCore 0:
  614.6 839.3 all-reduce.9
  1462.7 74.3 all-reduce.11
  1539.5 53.2 all-gather.7
  1595.0 107.8 all-gather.5
  1705.3 136.2 all-gather.9
  1843.8 136.2 all-gather.11
where the time goes:
time: 2010 us; the launch traced here: 2000 us
  waiting for transfers between devices  1200 us (60%)
  matrix products  299 us (15%)
  local copies, waits for them, and re-layouts  243 us (12%)
  other arithmetic  156 us (8%)
  blocking collectives  77.1 us (4%)
    unnamed x7, waiting for transfers between devices  836 us
    all_gather x1, waiting for transfers between devices, body(): lax.all_gather(merged[2], 'dp', axis=0, tiled=True)  130 us
    all_gather x1, waiting for transfers between devices, body(): lax.all_gather(merged[3], 'dp', axis=0, tiled=True)  128 us
    psum x1, waiting for transfers between devices, body(): lax.psum((weighting * shares[0], weighting * shares[1], weighting * share...  74.4 us
    dynamic_update_slice x4, local copies, waits for them, and re-layouts, body(): lax.map(forward_block, jnp.arange(block_count, dtype=jnp.int32))  65.9 us
    dot_general x1, matrix products, body(): jnp.dot(c_low, fc1_weight, preferred_element_type=jnp.float32) + fc1_bias  48.4 us
    convert_element_type x2, other arithmetic, attend_backward(): score_low = (probs * (prob_grad - delta_sum)).astype(jnp.bfloat16)  44.2 us
  transfers between devices with their start and end apart: 6, of which 5 were waited for; matrix products, arithmetic and copies ran while one was open for 4% of the time, Pallas kernels for 0%

commit v1 on v0

--- a/solution.py
+++ b/solution.py
@@ -1,9 +1,15 @@
+import functools
+import heapq
 import math
 
 import jax
 import jax.numpy as jnp
 from jax import lax
+from jax.experimental import pallas as pl
+from jax.experimental.pallas import tpu as pltpu
 from jax.sharding import PartitionSpec as P
+
+MESH = pl.DeviceIdType.MESH
 
 HEADS = 12
 HD = 64
@@ -12,6 +18,231 @@
 
 EPSILON = 1e-06
 MASKED = -1e30
+
+
+def halve(shape):
+    rows, cols = shape
+    if rows % 16 == 0: return 0
+    if cols % 256 == 0: return 1
+    return None
+
+def level_orders(nb, nd):
+    bk=[("bucket",i) for i in range(int(math.log2(nb)))]
+    dp=[("dp",i) for i in range(int(math.log2(nd)))]
+    rest_b=bk[1:]
+    a=bk[:1]+dp[:2]+rest_b+dp[2:]
+    b=bk[:1]+rest_b+dp[1:2]+dp[:1]+dp[2:]
+    return a,b
+
+def rate(bit):
+    if bit==("bucket",0): return 600e3
+    if bit==("dp",2): return 23e3
+    return 46e3
+def resource(bit):
+    if bit==("dp",2): return ("dp",1)
+    return bit
+
+class Job: pass
+
+def make_jobs(chunks, nb, nd):
+    orders=level_orders(nb,nd)
+    jobs=[]
+    for ci,(g,r0,rows,cols,ready) in enumerate(chunks):
+        for p in range(2):
+            if rows%16:
+                if p==1: continue
+                base,n=r0,rows
+            else:
+                n=rows//2; base=r0+p*n
+            j=Job(); j.g=g; j.base=base; j.shape=(n,cols); j.ready=ready; j.levels=[]
+            sh=(n,cols)
+            for bit in orders[p]:
+                d=halve(sh)
+                out=list(sh)
+                if d is not None: out[d]//=2
+                j.levels.append((bit,d,tuple(sh),tuple(out)))
+                sh=tuple(out)
+            jobs.append(j)
+    return jobs
+
+def simulate(jobs):
+    free={}
+    ev=[]
+    heap=[(j.ready,k,0) for k,j in enumerate(jobs)]
+    heapq.heapify(heap)
+    order=[]
+    while heap:
+        t,k,s=heapq.heappop(heap)
+        j=jobs[k]; L=len(j.levels)
+        lv = s if s<L else 2*L-1-s
+        bit,d,before,after=j.levels[lv]
+        moved=after if (s<L or d is not None) else None
+        size=4*after[0]*after[1] if moved else 0
+        if size==0:
+            end=t
+        else:
+            r=resource(bit)
+            start=max(t,free.get(r,0.0))
+            end=start+size/rate(bit)
+            free[r]=end
+            end+=2.0
+        order.append((end,t,k,s))
+        if s+1<2*L: heapq.heappush(heap,(end,k,s+1))
+    order.sort()
+    return [(k,s) for _,_,k,s in order], max(o[0] for o in order), order
+
+def bit_of(bit):
+    axis,i=bit
+    return (lax.axis_index(axis)//(1<<i))%2
+
+def partner(bit, names=("bucket","dp")):
+    axis,i=bit
+    me=lax.axis_index(axis)
+    other=me+(1-2*bit_of(bit))*(1<<i)
+    return tuple(other if n==axis else lax.axis_index(n) for n in names)
+
+def region(ref, off, shape):
+    r,c=off
+    if isinstance(c,int) and c==0 and ref.shape[1]==shape[1]:
+        return ref.at[pl.ds(r if isinstance(r,int) else pl.multiple_of(r,8),shape[0]),:]
+    return ref.at[pl.ds(r if isinstance(r,int) else pl.multiple_of(r,8),shape[0]),pl.ds(c if isinstance(c,int) else pl.multiple_of(c,128),shape[1])]
+
+def add_into(acc, off, recv, shape):
+    rows,cols=shape
+    rb=8
+    while rows%(rb*2)==0 and rb*2*cols<=32*1024: rb*=2
+    r,c=off
+    def one(i,_):
+        a=acc.at[pl.ds(pl.multiple_of(r+i*rb,8),rb), pl.ds(c if isinstance(c,int) else pl.multiple_of(c,128),cols)]
+        a[...]=a[...]+recv[pl.ds(pl.multiple_of(i*rb,8),rb),:]
+        return 0
+    lax.fori_loop(0,rows//rb,one,0)
+
+class Run:
+    def __init__(self, j, src, out, acc, recv, ss, rs, ls):
+        self.j=j; self.src=src; self.out=out; self.acc=acc; self.recv=recv
+        self.ss=ss; self.rs=rs; self.ls=ls
+        self.off=(0,0)
+        self.sends=[]
+        self.cp=None
+        self.loc=None
+        bit,d,before,after=j.levels[0]
+        self.ob=j.base
+        self.gofs=(j.base,0)
+    def split(self, lv, off):
+        bit,d,before,after=self.j.levels[lv]
+        b=bit_of(bit)
+        keep=list(off); send=list(off)
+        keep[d]=off[d]+b*after[d]; send[d]=off[d]+(1-b)*after[d]
+        return tuple(keep),tuple(send)
+    def start(self, s):
+        L=len(self.j.levels)
+        if s<L:
+            bit,d,before,after=self.j.levels[s]
+            if s==0:
+                assert d is not None
+                keep,send=self.split(0,(self.j.base,0))
+                self.gofs=keep
+                src=region(self.src,send,after)
+                self.loc=pltpu.make_async_copy(region(self.src,keep,after),self.acc,self.ls.at[0])
+                self.loc.start()
+                self.off=(0,0)
+            elif d is None:
+                src=region(self.acc,self.off,after)
+            else:
+                keep,send=self.split(s,self.off)
+                src=region(self.acc,send,after)
+                self.off=keep
+            cp=pltpu.make_async_remote_copy(src_ref=src,dst_ref=self.recv[s],send_sem=self.ss.at[s],recv_sem=self.rs.at[s],device_id=partner(bit),device_id_type=MESH)
+            cp.start()
+            self.cp=cp
+            if d is not None: self.sends.append(cp)
+        else:
+            lv=2*L-1-s
+            bit,d,before,after=self.j.levels[lv]
+            if s==L:
+                g=self.g()
+                self.piece=(g,after)
+                self.loc=pltpu.make_async_copy(region(self.acc,self.off,after),region(self.out,g,after),self.ls.at[1])
+                self.loc.start()
+                self.first=True
+            if d is None:
+                self.cp=None
+                return
+            g,shape=self.piece
+            assert shape==after,(shape,after)
+            if self.first:
+                src=region(self.acc,self.off,after)
+                self.first=False
+            else:
+                if self.loc is not None:
+                    self.loc.wait(); self.loc=None
+                src=region(self.out,g,after)
+            cp=pltpu.make_async_remote_copy(src_ref=src,dst_ref=region(self.out,g,after),send_sem=self.ss.at[s],recv_sem=self.rs.at[s],device_id=partner(bit),device_id_type=MESH)
+            cp.start(); self.cp=cp; self.sends.append(cp)
+    def g(self):
+        return (self.gofs[0]+self.off[0], self.gofs[1]+self.off[1])
+    def finish(self, s):
+        L=len(self.j.levels)
+        if s<L:
+            bit,d,before,after=self.j.levels[s]
+            if s==0:
+                self.loc.wait(); self.loc=None
+            if d is None: self.cp.wait()
+            else: self.cp.wait_recv()
+            add_into(self.acc,self.off,self.recv[s],after)
+        else:
+            lv=2*L-1-s
+            bit,d,before,after=self.j.levels[lv]
+            if self.cp is not None:
+                self.cp.wait_recv()
+            if d is not None:
+                g,_=self.piece
+                up=list(g); up[d]=g[d]-bit_of(bit)*after[d]
+                self.piece=(tuple(up),before)
+    def close(self):
+        if self.loc is not None: self.loc.wait()
+        for cp in self.sends: cp.wait_send()
+
+def barrier(bits):
+    sem=pltpu.get_barrier_semaphore()
+    for bit in bits:
+        pl.semaphore_signal(sem,inc=1,device_id=partner(bit),device_id_type=MESH)
+    pl.semaphore_wait(sem,len(bits))
+
+def scratch_of(jobs):
+    out=[]
+    for j in jobs:
+        out.append(pltpu.VMEM(j.levels[0][3],jnp.float32))
+        for bit,d,before,after in j.levels: out.append(pltpu.VMEM(after,jnp.float32))
+        L=len(j.levels)
+        out += [pltpu.SemaphoreType.DMA((2*L,)),pltpu.SemaphoreType.DMA((2*L,)),pltpu.SemaphoreType.DMA((2,))]
+    return out
+
+def ar_body(jobs, order, nin, bits, *refs):
+    ins=refs[:nin]; outs=refs[nin:2*nin]; sc=list(refs[2*nin:])
+    runs=[]
+    for j in jobs:
+        acc=sc.pop(0); recv=[sc.pop(0) for _ in j.levels]; ss,rs,ls=sc.pop(0),sc.pop(0),sc.pop(0)
+        runs.append(Run(j,ins[j.g],outs[j.g],acc,recv,ss,rs,ls))
+    barrier(bits)
+    for r in runs: r.start(0)
+    for k,s in order:
+        runs[k].finish(s)
+        if s+1<2*len(jobs[k].levels): runs[k].start(s+1)
+    for r in runs: r.close()
+
+def all_reduce(grads, chunks, nb, nd, cid=7):
+    jobs=make_jobs(chunks,nb,nd)
+    order,_,_=simulate(jobs)
+    bits=level_orders(nb,nd)[0]
+    n=len(grads)
+    return pl.pallas_call(functools.partial(ar_body,jobs,order,n,bits),
+        out_shape=tuple(jax.ShapeDtypeStruct(g.shape,jnp.float32) for g in grads),
+        in_specs=[pl.BlockSpec(memory_space=pltpu.HBM)]*n,
+        out_specs=tuple([pl.BlockSpec(memory_space=pltpu.HBM)]*n),
+        scratch_shapes=scratch_of(jobs),
+        compiler_params=pltpu.CompilerParams(collective_id=cid,has_side_effects=True,vmem_limit_bytes=60<<20),name="allreduce")(*grads)
 
 
 def norm_forward(values, gains, shifts):
@@ -195,39 +426,24 @@
         jnp.where(jnp.arange(counts.shape[0]) == lax.axis_index("bucket"), counts, 0.0)
     )
     weighting = own_count / (jnp.sum(counts) * math.sqrt(row_count * lax.axis_size("dp")))
-    flat_terms = (
-        qkv_w_term.reshape(-1),
-        out_w_term.reshape(-1),
-        fc1_w_term.reshape(-1),
-        fc2_w_term.reshape(-1),
-        small_terms,
-    )
-    shares = (
-        lax.psum_scatter(flat_terms[0], "dp", scatter_dimension=0, tiled=True),
-        lax.psum_scatter(flat_terms[1], "dp", scatter_dimension=0, tiled=True),
-        lax.psum_scatter(flat_terms[2], "dp", scatter_dimension=0, tiled=True),
-        lax.psum_scatter(flat_terms[3], "dp", scatter_dimension=0, tiled=True),
-        lax.psum_scatter(flat_terms[4], "dp", scatter_dimension=0, tiled=True),
-    )
-    merged = lax.psum(
-        (
-            weighting * shares[0],
-            weighting * shares[1],
-            weighting * shares[2],
-            weighting * shares[3],
-            weighting * shares[4],
-        ),
-        "bucket",
-    )
-    finished = (
-        lax.all_gather(merged[0], "dp", axis=0, tiled=True),
-        lax.all_gather(merged[1], "dp", axis=0, tiled=True),
-        lax.all_gather(merged[2], "dp", axis=0, tiled=True),
-        lax.all_gather(merged[3], "dp", axis=0, tiled=True),
-        lax.all_gather(merged[4], "dp", axis=0, tiled=True),
-    )
+    small_rows = small_terms.size // 128
+    small_pad = jnp.pad(small_terms.reshape(small_rows, 128), ((0, 128 - small_rows), (0, 0)))
+    terms = [
+        weighting * fc2_w_term,
+        weighting * fc1_w_term,
+        weighting * out_w_term,
+        weighting * qkv_w_term,
+        weighting * small_pad,
+    ]
+    wide = features // 4
+    chunks = [(0, 4 * wide * i, 4 * wide, features, 0.0) for i in range(4)]
+    chunks += [(1, wide * i, wide, 4 * features, 0.0) for i in range(4)]
+    chunks += [(2, 0, features, features, 0.0)]
+    chunks += [(3, 2 * wide * i, 2 * wide, 3 * features, 0.0) for i in range(2)]
+    chunks += [(4, 0, 128, 128, 0.0)]
+    finished = all_reduce(terms, chunks, lax.axis_size("bucket"), lax.axis_size("dp"))
     hidden_units = fc1_weight.shape[1]
-    small_done = finished[4]
+    small_done = finished[4][:small_rows].reshape(-1)
     offset_one = 3 * features
     offset_two = offset_one + features
     offset_three = offset_two + hidden_units
@@ -238,13 +454,13 @@
     return (
         out,
         tokens_grad,
-        finished[0].reshape(features, 3 * features),
+        finished[3],
         small_done[:offset_one],
-        finished[1].reshape(features, features),
+        finished[2],
         small_done[offset_one:offset_two],
-        finished[2].reshape(features, hidden_units),
+        finished[1],
         small_done[offset_two:offset_three],
-        finished[3].reshape(hidden_units, features),
+        finished[0],
         small_done[offset_three:offset_four],
         small_done[offset_four:offset_five].reshape(2, features),
         small_done[offset_five:offset_six].reshape(2, features),

time: 2010 us -> 920 us (0.46)
  waiting for transfers between devices: 1200 us -> 0 us
  Pallas kernels: 0 us -> 255 us
  blocking collectives: 77.1 us -> 0 us
  local copies, waits for them, and re-layouts: 243 us -> 197 us
    unnamed x7 -> x0, waiting for transfers between devices: 836 us -> none
    all_gather x4 -> x0, waiting for transfers between devices: 290 us -> none  [the longest x1 130 us: body(): lax.all_gather(merged[2], 'dp', axis=0, tiled=True)]
    pallas_call x0 -> x1, Pallas kernels: none -> 255 us  [all_reduce(): pl.pallas_call(functools.partial(ar_body, jobs, order, n, bits), out_shap...]
    psum x1 -> x0, waiting for transfers between devices: 74.4 us -> none  [body(): lax.psum((weighting * shares[0], weighting * shares[1], weighting * share...]
    reshape x7 -> x0, local copies, waits for them, and re-layouts: 55.7 us -> none  [the longest x1 11.3 us: body(): finished[3].reshape(hidden_units, features)]
    unnamed x1 -> x0, blocking collectives: 39.3 us -> none
    all_gather x1 -> x0, blocking collectives: 31.1 us -> none  [body(): lax.all_gather(merged[4], 'dp', axis=0, tiled=True)]
    unnamed x141 -> x144, local copies, waits for them, and re-layouts: 35.9 us -> 43 us
  transfers between devices with their start and end apart: 6 -> 0, of which waited for: 5 -> 0; matrix products, arithmetic and copies ran while one was open for 4% -> 0% of each run, Pallas kernels for 0% -> 0%
where the time goes in v1:
time: 920 us; the launch traced here: 913 us
  matrix products  309 us (34%)
  Pallas kernels  255 us (28%)
  local copies, waits for them, and re-layouts  197 us (21%)
  other arithmetic  145 us (16%)
    pallas_call x1, Pallas kernels, all_reduce(): pl.pallas_call(functools.partial(ar_body, jobs, order, n, bits), out_shap...  255 us
    dynamic_update_slice x4, local copies, waits for them, and re-layouts, body(): lax.map(forward_block, jnp.arange(block_count, dtype=jnp.int32))  66.1 us
    dot_general x1, matrix products, body(): jnp.dot(c_low, fc1_weight, preferred_element_type=jnp.float32) + fc1_bias  47.8 us
    convert_element_type x2, other arithmetic, attend_backward(): score_low = (probs * (prob_grad - delta_sum)).astype(jnp.bfloat16)  44.2 us
    unnamed x144, local copies, waits for them, and re-layouts  43 us
    dot_general x2, matrix products, attend_backward(): jnp.einsum('ihd,jhd->hij', out_grad, value_rows, preferred_element_type=j...  36.1 us
    dot_general x2, matrix products, attend_forward(): jnp.einsum('ihd,jhd->hij', query_rows, key_rows, preferred_element_type=j...  27.3 us
    dot_general x2, matrix products, attend_backward(): jnp.einsum('ihd,jhd->hij', query_rows, key_rows, preferred_element_type=j...  26.9 us

profile of v1, /device:TPU:0, one launch (start us, length us, event | category | flops | bytes accessed | tf_op | source)
XLA Modules:
  0.0 912.5 jit_solution(3533939352254134178)
XLA Ops:
  47.6 78.4 %while.27 = (s32[]{:T(128)}, bf16[2,512,12,64]{1,3,2,0:T(8,128)(2,1)}, f32[2,12,512,1]{2,1,3,0:T(8,128)}, s32[2]{0:T(128)S(1)}, s32[1024]{0:T(1024)S(1)}, /*inde...) while((s32[]{:T(128)}, ...), condition=%wide.region_9.10_spmd, body=%wide.region_6.9_spmd.sunk | while | flops 1661462528 | bytes 102615360 | solution.py:338
  49.6 13.6 %select_reduce_fusion.2 = (f32[12,512]{1,0:T(8,128)S(1)}, f32[12,512,1024]{2,1,0:T(8,128)}) fusion(pred[512,1024]{1,0:T(8,128)(4,1)S(1)} %broadcast_compare_fusion.4, bf16[1024,12,64]{0,2,1:T(8,128)(2,1)} %get-tuple-element.465, bf16[1024,12,64]{0,2,1:T(8,128)(2,1)} %get-tuple-element.464, s32[]{:T(128)S(6)} %select_n.53), kind=kOutput, calls=%fused_computation.2.clone.1 | convolution fusion | flops 817883136 | bytes 28073988 | tf_op jit(solution)/shard_map/while/body/eval_jaxpr/ihd,jhd->hij/dot_general | solution.py:266
  63.2 11.6 %exponential_reduce_fusion.2 = f32[12,512]{1,0:T(8,128)S(1)} fusion(f32[12,512,1024]{2,1,0:T(8,128)} %get-tuple-element.418, f32[12,512]{1,0:T(8,128)S(1)} %get-tuple-element.419, pred[512,1024]{1,0:T(8,128)(4,1)S(1)} %broadcast_compare_fusion.4), kind=kLoop, calls=%fused_computation.1.clone.1 | loop fusion | flops 18868224 | bytes 25739264 | tf_op jit(solution)/shard_map/while/body/eval_jaxpr/reduce_sum | solution.py:270
  74.9 10.9 %bitcast_dynamic-update-slice_fusion.5 = bf16[2,512,12,64]{1,3,2,0:T(8,128)(2,1)S(1)} fusion(bf16[2,512,12,64]{1,3,2,0:T(8,128)(2,1)S(1)} %copy-done.28, s32[]{:T(128)} %get-tuple-element.447, bf16[1024,12,64]{0,2,1:T(8,128)(2,1)S(1)} %copy-done.6, f32[12,512,1024]{2,1,0:T(8,128)} %get-tuple-element.418, f32[12,512]{1,0:T(8,128)S(1)} %get-tuple-element.420, ...), kind=kOutput, calls=%fused_computation.5.clone.1 | convolution fusion | flops 824180736 | bytes 28868612 | tf_op jit(solution)/shard_map/while/body/eval_jaxpr/hij,jhd->ihd/dot_general | solution.py:272
  88.7 13.6 %select_reduce_fusion.2 = (f32[12,512]{1,0:T(8,128)S(1)}, f32[12,512,1024]{2,1,0:T(8,128)}) fusion(pred[512,1024]{1,0:T(8,128)(4,1)S(1)} %broadcast_compare_fusion.4, bf16[1024,12,64]{0,2,1:T(8,128)(2,1)} %get-tuple-element.465, bf16[1024,12,64]{0,2,1:T(8,128)(2,1)} %get-tuple-element.464, s32[]{:T(128)S(6)} %select_n.53), kind=kOutput, calls=%fused_computation.2.clone.1 | convolution fusion | flops 817883136 | bytes 28073988 | tf_op jit(solution)/shard_map/while/body/eval_jaxpr/ihd,jhd->hij/dot_general | solution.py:266
  102.3 11.6 %exponential_reduce_fusion.2 = f32[12,512]{1,0:T(8,128)S(1)} fusion(f32[12,512,1024]{2,1,0:T(8,128)} %get-tuple-element.418, f32[12,512]{1,0:T(8,128)S(1)} %get-tuple-element.419, pred[512,1024]{1,0:T(8,128)(4,1)S(1)} %broadcast_compare_fusion.4), kind=kLoop, calls=%fused_computation.1.clone.1 | loop fusion | flops 18868224 | bytes 25739264 | tf_op jit(solution)/shard_map/while/body/eval_jaxpr/reduce_sum | solution.py:270
  114.0 10.9 %bitcast_dynamic-update-slice_fusion.5 = bf16[2,512,12,64]{1,3,2,0:T(8,128)(2,1)S(1)} fusion(bf16[2,512,12,64]{1,3,2,0:T(8,128)(2,1)S(1)} %copy-done.28, s32[]{:T(128)} %get-tuple-element.447, bf16[1024,12,64]{0,2,1:T(8,128)(2,1)S(1)} %copy-done.6, f32[12,512,1024]{2,1,0:T(8,128)} %get-tuple-element.418, f32[12,512]{1,0:T(8,128)S(1)} %get-tuple-element.420, ...), kind=kOutput, calls=%fused_computation.5.clone.1 | convolution fusion | flops 824180736 | bytes 28868612 | tf_op jit(solution)/shard_map/while/body/eval_jaxpr/hij,jhd->ihd/dot_general | solution.py:272
  133.4 47.8 %fusion.27 = (bf16[1024,3072]{1,0:T(8,128)(2,1)}, f32[1024,3072]{1,0:T(8,128)}) fusion(f32[3072]{0:T(1024)S(1)} %copy-done.65, bf16[768,3072]{1,0:T(8,128)(2,1)S(1)} %bitcast.155, f32[1024,768]{0,1:T(8,128)S(1)} %get-tuple-element.294, f32[768]{0:T(1024)S(1)} %copy-done.55, f32[768]{0:T(1024)S(1)} %copy-done.45, f32[1024]{0:T(1024)S(1)} %add_rsqrt_fusion.2, ...), kind=kOutput, calls=%fused_computation.41 | convolution fusion | flops 5043388416 | bytes 26765312 | tf_op jit(solution)/shard_map/dot_general | solution.py:343
  184.5 14.3 %convert_reduce_fusion = (f32[3072]{0:T(1024)}, bf16[1024,3072]{1,0:T(8,128)(2,1)S(1)}) fusion(f32[1024,3072]{1,0:T(8,128)} %get-tuple-element.296, f32[3072]{0:T(1024)} %param.30, bf16[3072,768]{1,0:T(8,128)(2,1)} %param.31, bf16[1024,768]{0,1:T(8,128)(2,1)} %copy.56, f32[1024]{0:T(1024)} %convert_element_type.73), kind=kOutput, calls=%fused_computation.48 | convolution fusion | flops 4875088896 | bytes 25194496 | tf_op jit(solution)/shard_map/td,fd->tf/dot_general | solution.py:352
  198.8 11.9 %fusion.71 = (f32[768]{0:T(1024)}, f32[1024,768]{1,0:T(8,128)}) fusion(bf16[1024,3072]{1,0:T(8,128)(2,1)S(1)} %get-tuple-element.298, bf16[768,3072]{1,0:T(8,128)(2,1)} %param.29), kind=kOutput, calls=%fused_computation.162 | convolution fusion | flops 4832623616 | bytes 14158848 | tf_op jit(solution)/shard_map/tf,df->td/dot_general | solution.py:359
  225.4 244.4 %while.28 = (s32[]{:T(128)}, f32[1024,12,64]{0,2,1:T(8,128)}, f32[1024,12,64]{0,2,1:T(8,128)}, f32[2,512,12,64]{1,0,3,2:T(2,128)}, s32[2]{0:T(128)S(1)}, /*index...) while((s32[]{:T(128)}, f32[1024,12,64]{0,2,1:T(8,128)}, ...), condition=%wide.region_16.17_spmd.clone, body=%wide.region_14.16_spmd.clone.sunk | while | flops 4105693184 | bytes 228034928 | solution.py:383
  226.7 13.4 %fusion.116 = f32[12,512,1024]{2,1,0:T(8,128)} fusion(bf16[1024,12,64]{0,2,1:T(8,128)(2,1)} %get-tuple-element.508, bf16[1024,12,64]{0,2,1:T(8,128)(2,1)} %get-tuple-element.506, s32[]{:T(128)S(6)} %select_n.57), kind=kOutput, calls=%fused_computation.29.clone.1 | convolution fusion | flops 805306368 | bytes 27525124 | tf_op jit(solution)/shard_map/while/body/eval_jaxpr/ihd,jhd->hij/dot_general | solution.py:279
  242.0 18.0 %multiply_reduce_fusion.16 = (f32[12,512]{1,0:T(8,128)}, f32[12,512,1024]{2,1,0:T(8,128)}) fusion(f32[12,512,1024]{2,1,0:T(8,128)} %fusion.116, f32[12,512]{1,0:T(8,128)} %dynamic-slice_bitcast_fusion.2, pred[512,1024]{1,0:T(8,128)(4,1)} %broadcast_compare_fusion.5, bf16[1024,12,64]{0,2,1:T(8,128)(2,1)} %get-tuple-element.511, ...), kind=kOutput, calls=%fused_computation.14.clone.1 | convolution fusion | flops 830466048 | bytes 53272580 | tf_op jit(solution)/shard_map/while/body/eval_jaxpr/ihd,jhd->hij/dot_general | solution.py:284
  260.0 22.1 %multiply_convert_fusion.6 = bf16[12,512,1024]{2,1,0:T(8,128)(2,1)} fusion(f32[12,512,1024]{2,1,0:T(8,128)} %get-tuple-element.433, f32[12,512,1024]{2,1,0:T(8,128)} %fusion.116, f32[12,512]{1,0:T(8,128)} %get-tuple-element.434, f32[12,512]{1,0:T(8,128)} %dynamic-slice_bitcast_fusion.2, pred[512,1024]{1,0:T(8,128)(4,1)} %broadcast_compare_fusion.5), kind=kLoop, calls=%fused_computation.13.clone.1 | loop fusion | flops 31457280 | bytes 63488000 | tf_op jit(solution)/shard_map/while/body/eval_jaxpr/convert_element_type | solution.py:286
  296.5 28.8 %dynamic_update_slice.19 = f32[2,512,12,64]{1,0,3,2:T(2,128)} dynamic-update-slice(f32[2,512,12,64]{1,0,3,2:T(2,128)} %get-tuple-element.489, f32[1,512,12,64]{1,0,3,2:T(1,128)} %copy.114, s32[]{:T(128)} %get-tuple-element.486, s32[]{:T(128)} %constant.67.clone.1..sunk.1, s32[]{:T(128)} %constant.67.clone.1..sunk.1, s32[]{:T(128)} %constant.67.clone.1..sunk.1) | dynamic-update-slice | bytes 3145732 | tf_op jit(solution)/shard_map/while/body/jit(dynamic_update_index_in_dim)/dynamic_update_slice | solution.py:338
  334.2 12.4 %bitcast_add_fusion.5 = f32[1024,12,64]{0,2,1:T(8,128)} fusion(f32[1024,12,64]{0,2,1:T(8,128)} %get-tuple-element.488, f32[12,512,1024]{2,1,0:T(8,128)} %fusion.116, f32[12,512]{1,0:T(8,128)S(1)} %copy-done.14, pred[512,1024]{1,0:T(8,128)(4,1)S(1)} %copy-done.2, pred[]{:T(512)S(6)} %compare.4, bf16[1024,12,64]{0,2,1:T(8,128)(2,1)S(1)} %copy-done.9, ...), kind=kOutput, calls=%fused_computation.21.clone.1 | convolution fusion | flops 825753600 | bytes 32800772 | tf_op jit(solution)/shard_map/while/body/eval_jaxpr/hij,ihd->jhd/dot_general | solution.py:283
  347.7 13.4 %fusion.116 = f32[12,512,1024]{2,1,0:T(8,128)} fusion(bf16[1024,12,64]{0,2,1:T(8,128)(2,1)} %get-tuple-element.508, bf16[1024,12,64]{0,2,1:T(8,128)(2,1)} %get-tuple-element.506, s32[]{:T(128)S(6)} %select_n.57), kind=kOutput, calls=%fused_computation.29.clone.1 | convolution fusion | flops 805306368 | bytes 27525124 | tf_op jit(solution)/shard_map/while/body/eval_jaxpr/ihd,jhd->hij/dot_general | solution.py:279
  363.0 18.0 %multiply_reduce_fusion.16 = (f32[12,512]{1,0:T(8,128)}, f32[12,512,1024]{2,1,0:T(8,128)}) fusion(f32[12,512,1024]{2,1,0:T(8,128)} %fusion.116, f32[12,512]{1,0:T(8,128)} %dynamic-slice_bitcast_fusion.2, pred[512,1024]{1,0:T(8,128)(4,1)} %broadcast_compare_fusion.5, bf16[1024,12,64]{0,2,1:T(8,128)(2,1)} %get-tuple-element.511, ...), kind=kOutput, calls=%fused_computation.14.clone.1 | convolution fusion | flops 830466048 | bytes 53272580 | tf_op jit(solution)/shard_map/while/body/eval_jaxpr/ihd,jhd->hij/dot_general | solution.py:284
  381.1 22.1 %multiply_convert_fusion.6 = bf16[12,512,1024]{2,1,0:T(8,128)(2,1)} fusion(f32[12,512,1024]{2,1,0:T(8,128)} %get-tuple-element.433, f32[12,512,1024]{2,1,0:T(8,128)} %fusion.116, f32[12,512]{1,0:T(8,128)} %get-tuple-element.434, f32[12,512]{1,0:T(8,128)} %dynamic-slice_bitcast_fusion.2, pred[512,1024]{1,0:T(8,128)(4,1)} %broadcast_compare_fusion.5), kind=kLoop, calls=%fused_computation.13.clone.1 | loop fusion | flops 31457280 | bytes 63488000 | tf_op jit(solution)/shard_map/while/body/eval_jaxpr/convert_element_type | solution.py:286
  417.5 28.8 %dynamic_update_slice.19 = f32[2,512,12,64]{1,0,3,2:T(2,128)} dynamic-update-slice(f32[2,512,12,64]{1,0,3,2:T(2,128)} %get-tuple-element.489, f32[1,512,12,64]{1,0,3,2:T(1,128)} %copy.114, s32[]{:T(128)} %get-tuple-element.486, s32[]{:T(128)} %constant.67.clone.1..sunk.1, s32[]{:T(128)} %constant.67.clone.1..sunk.1, s32[]{:T(128)} %constant.67.clone.1..sunk.1) | dynamic-update-slice | bytes 3145732 | tf_op jit(solution)/shard_map/while/body/jit(dynamic_update_index_in_dim)/dynamic_update_slice | solution.py:338
  456.1 13.3 %bitcast_add_fusion.5 = f32[1024,12,64]{0,2,1:T(8,128)} fusion(f32[1024,12,64]{0,2,1:T(8,128)} %get-tuple-element.488, f32[12,512,1024]{2,1,0:T(8,128)} %fusion.116, f32[12,512]{1,0:T(8,128)S(1)} %copy-done.14, pred[512,1024]{1,0:T(8,128)(4,1)S(1)} %copy-done.2, pred[]{:T(512)S(6)} %compare.4, bf16[1024,12,64]{0,2,1:T(8,128)(2,1)S(1)} %copy-done.9, ...), kind=kOutput, calls=%fused_computation.21.clone.1 | convolution fusion | flops 825753600 | bytes 32800772 | tf_op jit(solution)/shard_map/while/body/eval_jaxpr/hij,ihd->jhd/dot_general | solution.py:283
  478.4 10.7 %multiply_reduce_fusion.2 = (f32[64]{0:T(128)}, f32[2,512,12]{1,0,2:T(2,128)}, f32[2,512,12]{1,0,2:T(2,128)S(1)}, f32[64]{0:T(128)}) fusion(f32[2,512,12,64]{1,0,3,2:T(2,128)} %get-tuple-element.123, f32[2,512,12,64]{1,0,3,2:T(2,128)} %reshape.299, f32[2,512,12]{1,0,2:T(2,128)} %rsqrt.40, f32[2,512,12]{1,0,2:T(2,128)} %div.89, ...), kind=kLoop, calls=%fused_computation.90 | loop fusion | flops 7839616 | bytes 6488832 | tf_op jit(solution)/shard_map/reduce_sum | solution.py:389
  577.2 10.7 %convolution_multiply_fusion.1.refs_1_ = f32[768,3072]{1,0:T(8,128)} fusion(bf16[1024,3072]{1,0:T(8,128)(2,1)} %copy-done.68, f32[]{:T(128)S(6)} %div.96, f32[1024,768]{0,1:T(8,128)S(1)} %copy-done.12, f32[768]{0:T(1024)S(1)} %copy-done.56, f32[768]{0:T(1024)S(1)} %copy-done.46, f32[1024]{0:T(1024)S(1)} %copy-done.48, f32[1024]{0:T(1024)S(1)} %copy-done.40), kind=kOutput, calls=%fused_computation.67 | convolution fusion | flops 4838129664 | bytes 18888708 | tf_op jit(solution)/shard_map/td,tf->df/dot_general | solution.py:357
  601.2 254.8 %allreduce.1 = (f32[3072,768]{1,0:T(8,128)}, f32[768,3072]{1,0:T(8,128)}, f32[768,768]{1,0:T(8,128)}, f32[768,2304]{1,0:T(8,128)}, f32[128,128]{1,0:T(8,128)}) custom-call(f32[3072,768]{1,0:T(8,128)} %convolution_multiply_fusion.2.refs_0_, f32[768,3072]{1,0:T(8,128)} %convolution_multiply_fusion.1.refs_1_, f32[768,768]{1,0:T(8,128)} %convolution_multiply_fusion.3.refs_2_, ...), custom_call_target="tpu_custom_call" | custom-call | tf_op jit(solution)/shard_map/allreduce/pallas_call | solution.py:240
  (293 shorter events, 293.2 us)
Async XLA Ops:
  63.2 11.7 %copy-start.34 = (f32[2,12,512,1]{2,1,3,0:T(8,128)S(1)}, f32[2,12,512,1]{2,1,3,0:T(8,128)}, u32[]{:S(2)}) copy-start(f32[2,12,512,1]{2,1,3,0:T(8,128)} %get-tuple-element.449) | copy-start | bytes 147460 | tf_op jit(solution)/shard_map/while
  63.2 11.7 %copy-start.6 = (bf16[1024,12,64]{0,2,1:T(8,128)(2,1)S(1)}, bf16[1024,12,64]{0,2,1:T(8,128)(2,1)}, u32[]{:S(2)}) copy-start(bf16[1024,12,64]{0,2,1:T(8,128)(2,1)} %get-tuple-element.466) | copy-start | bytes 4718596 | tf_op jit(solution)/shard_map/while
  63.2 11.7 %copy-start.28 = (bf16[2,512,12,64]{1,3,2,0:T(8,128)(2,1)S(1)}, bf16[2,512,12,64]{1,3,2,0:T(8,128)(2,1)}, u32[]{:S(2)}) copy-start(bf16[2,512,12,64]{1,3,2,0:T(8,128)(2,1)} %get-tuple-element.448) | copy-start | bytes 4718596 | tf_op jit(solution)/shard_map/while
  74.9 10.9 %copy-start.35 = (f32[2,12,512,1]{2,1,3,0:T(8,128)}, f32[2,12,512,1]{2,1,3,0:T(8,128)S(1)}, u32[]{:S(2)}) copy-start(f32[2,12,512,1]{2,1,3,0:T(8,128)S(1)} %get-tuple-element.461) | copy-start | bytes 147460 | tf_op jit(solution)/shard_map/while
  102.3 11.7 %copy-start.34 = (f32[2,12,512,1]{2,1,3,0:T(8,128)S(1)}, f32[2,12,512,1]{2,1,3,0:T(8,128)}, u32[]{:S(2)}) copy-start(f32[2,12,512,1]{2,1,3,0:T(8,128)} %get-tuple-element.449) | copy-start | bytes 147460 | tf_op jit(solution)/shard_map/while
  102.3 11.7 %copy-start.6 = (bf16[1024,12,64]{0,2,1:T(8,128)(2,1)S(1)}, bf16[1024,12,64]{0,2,1:T(8,128)(2,1)}, u32[]{:S(2)}) copy-start(bf16[1024,12,64]{0,2,1:T(8,128)(2,1)} %get-tuple-element.466) | copy-start | bytes 4718596 | tf_op jit(solution)/shard_map/while
  102.3 11.7 %copy-start.28 = (bf16[2,512,12,64]{1,3,2,0:T(8,128)(2,1)S(1)}, bf16[2,512,12,64]{1,3,2,0:T(8,128)(2,1)}, u32[]{:S(2)}) copy-start(bf16[2,512,12,64]{1,3,2,0:T(8,128)(2,1)} %get-tuple-element.448) | copy-start | bytes 4718596 | tf_op jit(solution)/shard_map/while
  114.0 10.9 %copy-start.35 = (f32[2,12,512,1]{2,1,3,0:T(8,128)}, f32[2,12,512,1]{2,1,3,0:T(8,128)S(1)}, u32[]{:S(2)}) copy-start(f32[2,12,512,1]{2,1,3,0:T(8,128)S(1)} %get-tuple-element.461) | copy-start | bytes 147460 | tf_op jit(solution)/shard_map/while
  131.3 49.9 %copy-start.10 = (f32[1024,768]{0,1:T(8,128)}, f32[1024,768]{0,1:T(8,128)S(1)}, u32[]{:S(2)}) copy-start(f32[1024,768]{0,1:T(8,128)S(1)} %get-tuple-element.294) | copy-start | bytes 9437188
  131.4 87.5 %copy-start.39 = (f32[1024]{0:T(1024)}, f32[1024]{0:T(1024)S(1)}, u32[]{:S(2)}) copy-start(f32[1024]{0:T(1024)S(1)} %broadcast_multiply_fusion.8) | copy-start | bytes 12292
  131.8 87.1 %copy-start.47 = (f32[1024]{0:T(1024)}, f32[1024]{0:T(1024)S(1)}, u32[]{:S(2)}) copy-start(f32[1024]{0:T(1024)S(1)} %add_rsqrt_fusion.2) | copy-start | bytes 12292
  133.4 47.9 %copy-start.58 = (s32[1024]{0:T(1024)S(1)}, s32[1024]{0:T(1024)}, u32[]{:S(2)}) copy-start(s32[1024]{0:T(1024)} %param.23) | copy-start | bytes 12292
  198.8 11.9 %copy-start.68 = (bf16[1024,3072]{1,0:T(8,128)(2,1)}, bf16[1024,3072]{1,0:T(8,128)(2,1)S(1)}, u32[]{:S(2)}) copy-start(bf16[1024,3072]{1,0:T(8,128)(2,1)S(1)} %get-tuple-element.298) | copy-start | bytes 18874372
  226.7 14.7 %copy-start.36 = (f32[2,12,512,1]{2,1,3,0:T(8,128)S(1)}, f32[2,12,512,1]{2,1,3,0:T(8,128)}, u32[]{:S(2)}) copy-start(f32[2,12,512,1]{2,1,3,0:T(8,128)} %get-tuple-element.509) | copy-start | bytes 147460 | tf_op jit(solution)/shard_map/while
  347.7 14.7 %copy-start.36 = (f32[2,12,512,1]{2,1,3,0:T(8,128)S(1)}, f32[2,12,512,1]{2,1,3,0:T(8,128)}, u32[]{:S(2)}) copy-start(f32[2,12,512,1]{2,1,3,0:T(8,128)} %get-tuple-element.509) | copy-start | bytes 147460 | tf_op jit(solution)/shard_map/while
  567.1 10.1 %copy-start.40 = (f32[1024]{0:T(1024)S(1)}, f32[1024]{0:T(1024)}, u32[]{:S(2)}) copy-start(f32[1024]{0:T(1024)} %copy-done.39) | copy-start | bytes 12292
  567.1 10.1 %copy-start.46 = (f32[768]{0:T(1024)S(1)}, f32[768]{0:T(1024)}, u32[]{:S(2)}) copy-start(f32[768]{0:T(1024)} %get-tuple-element.304) | copy-start | bytes 9220
  567.1 10.1 %copy-start.48 = (f32[1024]{0:T(1024)S(1)}, f32[1024]{0:T(1024)}, u32[]{:S(2)}) copy-start(f32[1024]{0:T(1024)} %copy-done.47) | copy-start | bytes 12292
  567.1 10.1 %copy-start.56 = (f32[768]{0:T(1024)S(1)}, f32[768]{0:T(1024)}, u32[]{:S(2)}) copy-start(f32[768]{0:T(1024)} %get-tuple-element.232) | copy-start | bytes 9220
  577.2 10.8 %copy-start.17 = (f32[1024,768]{0,1:T(8,128)S(1)}, f32[1024,768]{0,1:T(8,128)}, u32[]{:S(2)}) copy-start(f32[1024,768]{0,1:T(8,128)} %copy-done.16) | copy-start | bytes 9437188
  577.2 10.7 %copy-start.27 = (bf16[96,8,2,512]{3,1,2,0:T(8,128)(2,1)S(1)}, bf16[96,8,2,512]{3,1,2,0:T(8,128)(2,1)}, u32[]{:S(2)}) copy-start(bf16[96,8,2,512]{3,1,2,0:T(8,128)(2,1)} %copy-done.26) | copy-start | bytes 4718596
  601.2 267.9 %copy-start.42 = (f32[768]{0:T(1024)S(1)}, f32[768]{0:T(1024)}, u32[]{:S(2)}) copy-start(f32[768]{0:T(1024)} %copy-done.41) | copy-start | bytes 9220
  601.2 267.9 %copy-start.44 = (f32[1024]{0:T(1024)S(1)}, f32[1024]{0:T(1024)}, u32[]{:S(2)}) copy-start(f32[1024]{0:T(1024)} %copy-done.43) | copy-start | bytes 12292
  897.8 10.7 %slice-start = ((s8[9437184]{0:T(1024)(128)(4,1)}), s8[4194304]{0:T(1024)(128)(4,1)S(1)}, s32[]{:S(2)}) async-start(s8[9437184]{0:T(1024)(128)(4,1)} %bitcast.142), calls=%async_computation | async-start | bytes 8388608
  (59 other events, 293.9 us)

commit v2 on v0

v2 whole, which is shorter than its diff:
```python
import functools
import heapq
import math

import jax
import jax.numpy as jnp
from jax import lax
from jax.experimental import pallas as pl
from jax.experimental.pallas import tpu as pltpu
from jax.sharding import PartitionSpec as P

F32=jnp.float32; BF=jnp.bfloat16
EPSILON=1e-6
NEG=-1e30
HD=64
VM=58<<20

def mm(a,b,ca=1,cb=0):
    return lax.dot_general(a,b,(((ca,),(cb,)),((),())),preferred_element_type=F32)

def row_norm(x):
    c=x-jnp.mean(x,axis=-1,keepdims=True)
    r=lax.rsqrt(jnp.mean(c*c,axis=-1,keepdims=True)+EPSILON)
    return c*r,r

def head_avg(x,m,twice):
    out=[]
    for i in range(x.shape[1]//256):
        part=x[:,256*i:256*(i+1)]
        hi=part.astype(BF)
        s=mm(hi,m)
        if twice: s=s+mm((part-hi.astype(F32)).astype(BF),m)
        out.append(s)
    return jnp.concatenate(out,axis=1)

def avg_matrix():
    i=lax.broadcasted_iota(jnp.int32,(256,256),0)//HD
    j=lax.broadcasted_iota(jnp.int32,(256,256),1)//HD
    return jnp.where(i==j,1.0/HD,0.0).astype(BF)

def whole(a):
    nd=len(a.shape)
    return pl.BlockSpec(a.shape,lambda *_:(0,)*nd,pipeline_mode=pl.Buffered(1))

def qkv_kernel(x,w,b,ng,ns,qg,qs,a_o,q_o,k_o,v_o,qu_o,ku_o,qr_o,kr_o):
    d=x.shape[1]
    u,_=row_norm(x[...].astype(F32))
    a=(u*ng[0:1,:]+ns[0:1,:]).astype(BF)
    a_o[...]=a
    m=avg_matrix()
    for i,(lo,un,rr) in enumerate(((q_o,qu_o,qr_o),(k_o,ku_o,kr_o))):
        raw=mm(a,w[:,i*d:(i+1)*d])+b[:,i*d:(i+1)*d]
        c=raw-head_avg(raw,m,True)
        r=lax.rsqrt(head_avg(c*c,m,False)+EPSILON)
        unit=c*r
        un[...]=unit.astype(BF)
        rr[...]=r
        n=unit*qg[i:i+1,:]+qs[i:i+1,:]
        if i==0: n=n*(1.0/math.sqrt(HD))
        lo[...]=n.astype(BF)
    v_o[...]=(mm(a,w[:,2*d:])+b[:,2*d:]).astype(BF)

def qkv_forward(x,w,b,ng,ns,qg,qs,rb=256):
    t,d=x.shape
    rows=pl.BlockSpec((rb,d),lambda i:(i,0))
    sh=lambda dt: jax.ShapeDtypeStruct((t,d),dt)
    return pl.pallas_call(qkv_kernel,grid=(t//rb,),
        in_specs=[rows,whole(w),whole(b),whole(ng),whole(ns),whole(qg),whole(qs)],
        out_specs=[rows]*8,
        out_shape=[sh(BF)]*6+[sh(F32)]*2,
        compiler_params=pltpu.CompilerParams(vmem_limit_bytes=VM),name="norm_qkv")(x,w,b,ng,ns,qg,qs)

def attend_kernel(q,k,v,sr,sc,o,lse,ob=256):
    t=q.shape[0]
    vt=v[...].T
    kk=k[...]
    lane=lax.broadcasted_iota(jnp.int32,(1,2*HD),1)//HD
    for i in range(t//ob):
        same=sc[...]==sr[:,i*ob:(i+1)*ob]
        parts=[]
        for h in range(2):
            qm=jnp.where(lane==h,q[i*ob:(i+1)*ob,:],0)
            s=jnp.where(same,mm(kk,qm,1,1),NEG)
            m=jnp.max(s,axis=0,keepdims=True)
            p=jnp.exp(s-m)
            l=jnp.sum(p,axis=0,keepdims=True)
            lse[0,h:h+1,i*ob:(i+1)*ob]=m+jnp.log(l)
            acc=mm(vt[h*HD:(h+1)*HD,:],p.astype(BF))
            parts.append(acc*(1.0/l))
        o[i*ob:(i+1)*ob,:]=jnp.concatenate(parts,axis=0).T.astype(BF)

def attend_forward(q,k,v,sr,sc):
    t,d=q.shape
    hp=d//(2*HD)
    col=pl.BlockSpec((t,2*HD),lambda h:(0,h))
    return pl.pallas_call(attend_kernel,grid=(hp,),
        in_specs=[col,col,col,whole(sr),whole(sc)],
        out_specs=[col,pl.BlockSpec((1,2,t),lambda h:(h,0,0))],
        out_shape=[jax.ShapeDtypeStruct((t,d),BF),jax.ShapeDtypeStruct((hp,2,t),F32)],
        compiler_params=pltpu.CompilerParams(vmem_limit_bytes=VM),name="attend")(q,k,v,sr,sc)

def mlp_kernel(nf,x,cot,live,attn,wo,bo,w1,b1,w2,b2,ng,ns,
               out_o,dhid_o,dattn_o,g_o,du_o,dm_o,c_o,db_o,small_o):
    i=pl.program_id(0)
    rb,d=x.shape
    hid=x[...].astype(F32)+mm(attn[...],wo[...])+bo[...]
    unit,r=row_norm(hid)
    c=(unit*ng[1:2,:]+ns[1:2,:]).astype(BF)
    c_o[...]=c
    lv=live[...].astype(F32)
    dm=cot[...].astype(F32)*lv
    dml=dm.astype(BF)
    dm_o[...]=dml
    out=jnp.zeros((rb,d),F32); dc=jnp.zeros((rb,d),F32)
    sums=[]
    for f in range(nf):
        cols=slice(f*d,(f+1)*d)
        pre=mm(c,w1[:,cols])+b1[:,cols]
        dg=mm(dml,w2[cols,:],1,1)
        phi=0.5*(1.0+lax.erf(pre*(1.0/math.sqrt(2.0))))
        g=(pre*phi).astype(BF)
        slope=phi+pre*jnp.exp(-0.5*pre*pre)*(1.0/math.sqrt(2.0*math.pi))
        du=(dg*slope).astype(BF)
        g_o[:,cols]=g
        du_o[:,cols]=du
        out=out+mm(g,w2[cols,:])
        dc=dc+mm(du,w1[:,cols],1,1)
        sums.append(jnp.sum(du.astype(F32),axis=0,keepdims=True))
    out_o[...]=(lv*(hid+out+b2[...])).astype(BF)
    e=dc*ng[1:2,:]
    dh=dm+r*(e-jnp.mean(e,axis=-1,keepdims=True)-unit*jnp.mean(e*unit,axis=-1,keepdims=True))
    dhid_o[...]=dh
    db=dh.astype(BF)
    db_o[...]=db
    dattn_o[...]=mm(db,wo[...],1,1).astype(BF)
    total=jnp.concatenate([jnp.sum(db.astype(F32),axis=0,keepdims=True)]+sums+[jnp.sum(dm,axis=0,keepdims=True),
        jnp.sum(dc*unit,axis=0,keepdims=True),jnp.sum(dc,axis=0,keepdims=True)],axis=0)
    @pl.when(i==0)
    def _(): small_o[...]=total
    @pl.when(i>0)
    def _(): small_o[...]+=total

def mlp(x,cot,live,attn,wo,bo,w1,b1,w2,b2,ng,ns,rb=256):
    t,d=x.shape; ff=w1.shape[1]; nf=ff//d
    rows=pl.BlockSpec((rb,d),lambda i:(i,0))
    wide=pl.BlockSpec((rb,ff),lambda i:(i,0))
    low=jax.ShapeDtypeStruct((t,d),BF)
    big=jax.ShapeDtypeStruct((t,ff),BF)
    return pl.pallas_call(functools.partial(mlp_kernel,nf),grid=(t//rb,),
        in_specs=[rows,rows,pl.BlockSpec((rb,1),lambda i:(i,0)),rows]+[whole(a) for a in (wo,bo,w1,b1,w2,b2,ng,ns)],
        out_specs=[rows,rows,rows,wide,wide,rows,rows,rows,pl.BlockSpec((nf+4,d),lambda i:(0,0))],
        out_shape=[low,jax.ShapeDtypeStruct((t,d),F32),low,big,big,low,low,low,jax.ShapeDtypeStruct((nf+4,d),F32)],
        compiler_params=pltpu.CompilerParams(vmem_limit_bytes=VM),name="mlp")(x,cot,live,attn,wo,bo,w1,b1,w2,b2,ng,ns)

MESH = pl.DeviceIdType.MESH
LATENCY=2.0
TICK=0.7

def halve(shape):
    rows, cols = shape
    if rows % 16 == 0: return 0
    if cols % 256 == 0: return 1
    return None

def bits_of(nb, nd):
    return ([("bucket",i) for i in range(int(math.log2(nb)))]
            + [("dp",i) for i in range(int(math.log2(nd)))])

def level_orders(nb, nd):
    bk=[("bucket",i) for i in range(int(math.log2(nb)))]
    dp=[("dp",i) for i in range(int(math.log2(nd)))]
    a=bk[:1]+dp[:2]+bk[1:]+dp[2:]
    b=bk[:1]+bk[1:]+dp[1:2]+dp[:1]+dp[2:]
    return a,b

class Job:
    def __init__(self, chunk, part, out, place, local, shape, order):
        self.chunk=chunk; self.part=part; self.out=out; self.place=place; self.local=local
        self.levels=[]
        for bit in order:
            d=halve(shape)
            after=list(shape)
            if d is not None: after[d]//=2
            self.levels.append((bit,d,tuple(shape),tuple(after)))
            shape=tuple(after)

def make_jobs(chunks, nb, nd):
    orders=level_orders(nb,nd)
    jobs=[]
    for c,(out,r,k,rows,cols) in enumerate(chunks):
        for p in range(2):
            local=p*(rows//2)
            jobs.append(Job(c,p,out,(r+local,k),local,(rows//2,cols),orders[p]))
    return jobs

class Links:
    def __init__(self): self.free={}
    def end(self, bit, size, t):
        if bit==("dp",2):
            mid,low=self.free.get(bit,0.0),self.free.get(("dp",1),0.0)
            start=max(t,mid,low)
            self.free[("dp",1)]=max(t,low)+size/46e3
            self.free[bit]=start+size/23e3
            return start+size/23e3+LATENCY
        rate=600e3 if bit==("bucket",0) else 46e3
        start=max(t,self.free.get(bit,0.0))
        self.free[bit]=start+size/rate
        return self.free[bit]+LATENCY

def schedule(jobs, steps, ring, shares):
    links=Links(); heap=[]; items=[]; done=set(); now=0.0
    of_chunk={}
    for k,j in enumerate(jobs): of_chunk.setdefault(j.chunk,[]).append(k)
    def issue(k,s,t):
        L=len(jobs[k].levels)
        bit,d,before,after=jobs[k].levels[s if s<L else 2*L-1-s]
        end=t if (s>=L and d is None) else links.end(bit,4*after[0]*after[1],t)
        heapq.heappush(heap,(end,k,s))
    def one(t):
        end,k,s=heapq.heappop(heap)
        t=max(t,end)+TICK
        items.append(("end",k,s)); done.add((k,s))
        if s+1<2*len(jobs[k].levels): issue(k,s+1,t)
        return t
    for i,(chunk,us) in enumerate(steps):
        while heap and heap[0][0]<=now: now=one(now)
        if chunk is not None:
            need=[(k,0) for k in of_chunk.get(chunk-ring,[])] if us>0 and chunk+1<len(of_chunk) else []
            if chunk in shares:
                need+=[(k,2*len(jobs[k].levels)-1) for k in of_chunk[shares[chunk]]]
            while not all(n in done for n in need): now=one(now)
        items.append(("step",i)); now+=us
        if chunk is not None:
            for k in of_chunk[chunk]: issue(k,0,now)
    while heap: now=one(now)
    return items,now

def bit_of(bit):
    axis,i=bit
    return (lax.axis_index(axis)//(1<<i))%2

def partner(bit):
    axis,i=bit
    me=lax.axis_index(axis)
    other=me+(1-2*bit_of(bit))*(1<<i)
    return tuple(other if n==axis else lax.axis_index(n) for n in ("bucket","dp"))

def span(start,size,by):
    return pl.ds(start if isinstance(start,int) else pl.multiple_of(start,by),size)

def region(ref, off, shape):
    return ref.at[span(off[0],shape[0],8),span(off[1],shape[1],128)]

def add_rows(dst, a, b, shape):
    rows,cols=shape
    rb=8
    while rows%(rb*2)==0 and rb*2*cols<=32*1024: rb*=2
    def one(i,_):
        at=pl.ds(pl.multiple_of(i*rb,8),rb)
        dst[at,:]=a[at,:]+b[at,:]
        return 0
    lax.fori_loop(0,rows//rb,one,0)

class Run:
    def __init__(self, job, src, out, acc, recv, ss, rs, ls, credit=None, give=False, take=False):
        self.j=job; self.src=src; self.out=out; self.acc=acc; self.recv=recv
        self.ss=ss; self.rs=rs; self.ls=ls
        self.credit=credit; self.give=give; self.take=take
        self.n=len(job.levels)
        self.unsent={s for s in range(2*self.n) if self.level(s)[1] is not None}
        self.stored=False
    def level(self, s):
        return self.j.levels[s if s<self.n else 2*self.n-1-s]
    def offset(self, first, last):
        off=[0,0]
        for bit,d,before,after in self.j.levels[first:last+1]:
            if d is not None: off[d]=off[d]+bit_of(bit)*after[d]
        return off
    def given(self, s, off):
        bit,d,before,after=self.j.levels[s]
        off=list(off); off[d]=off[d]+(1-bit_of(bit))*after[d]
        return off
    def piece(self, lv):
        off=self.offset(0,lv)
        return [self.j.place[0]+off[0],self.j.place[1]+off[1]]
    def local(self):
        after=self.level(self.n)[3]
        return pltpu.make_async_copy(region(self.acc,self.offset(1,self.n-1),after),
                                     region(self.out,self.piece(self.n-1),after),self.ls.at[0])
    def remote(self, s):
        bit,d,before,after=self.level(s)
        if s==0:
            src,dst=region(self.src,self.given(0,[self.j.local,0]),after),self.recv[0]
        elif s<self.n:
            off=self.offset(1,s-1)
            src,dst=region(self.acc,off if d is None else self.given(s,off),after),self.recv[s]
        else:
            dst=region(self.out,self.piece(2*self.n-1-s),after)
            first=all(self.level(i)[1] is None for i in range(self.n,s))
            src=region(self.acc,self.offset(1,self.n-1),after) if first else dst
        return pltpu.make_async_remote_copy(src_ref=src,dst_ref=dst,send_sem=self.ss.at[s],recv_sem=self.rs.at[s],
                                            device_id=partner(bit),device_id_type=MESH)
    def start(self, s):
        bit,d,before,after=self.level(s)
        if s==self.n: self.local().start()
        if s>=self.n and d is None: return
        if s>self.n and not self.stored and any(self.level(i)[1] is not None for i in range(self.n,s)):
            self.local().wait(); self.stored=True
        if s==0 and self.take: pl.semaphore_wait(self.credit,1)
        self.remote(s).start()
    def finish(self, s):
        bit,d,before,after=self.level(s)
        if s>=self.n:
            if d is not None: self.remote(s).wait_recv()
        else:
            if d is None: self.remote(s).wait()
            else: self.remote(s).wait_recv()
            to=region(self.acc,self.offset(1,s),after)
            own=region(self.src,[self.j.local+self.offset(0,0)[0],0],after) if s==0 else to
            add_rows(to,own,self.recv[s],after)
            if s==0 and self.give:
                pl.semaphore_signal(self.credit,inc=1,device_id=partner(bit),device_id_type=MESH)
        if s+1<2*self.n: self.start(s+1)
    def sent(self):
        if 0 in self.unsent: self.remote(0).wait_send(); self.unsent.discard(0)
    def close(self):
        if not self.stored: self.local().wait(); self.stored=True
        for s in sorted(self.unsent): self.remote(s).wait_send()
        self.unsent=set()

RING=2

def back_kernel(plan,*refs):
    (jobs,items,nchunk,nf,nhead,nblk,nrow,shares,bits)=plan
    refs=list(refs)
    def take(n):
        out=refs[:n]; del refs[:n]; return out
    (wt,g,du,dm,c,at_h,db,a,w)=take(9)
    (q,k,v,do,at,lse,qu,ku,qr,kr)=take(10)
    (sr,sc,qg,mid,x,dh,ng)=take(7)
    outs=take(5)
    (tg_o,)=take(1)
    (pool,stage,l0,dqkv,dq_s,dk_s,dv_s,kt_s,small)=take(9)
    (pool_sem,credit)=take(2)
    t,d=at_h.shape
    ob=t//nblk
    own=nchunk-len(shares)-1
    bufs=[]
    for n in range(own+1):
        pair=[]
        for p in range(2):
            L=len(jobs[2*(n if n<own else nchunk-1)+p].levels)
            pair.append((take(1)[0],take(L-1 if n<own else L)))
        bufs.append(pair)
    runs=[]
    for n,j in enumerate(jobs):
        ss,rs,ls=take(3)
        if j.chunk==nchunk-1:
            acc,recv=bufs[own][j.part]
            runs.append(Run(j,small,outs[j.out],acc,recv,ss,rs,ls))
        else:
            acc,recv=bufs[shares.get(j.chunk,j.chunk)][j.part]
            runs.append(Run(j,stage.at[j.chunk%RING],outs[j.out],acc,[l0.at[2*(j.chunk%RING)+j.part]]+list(recv),ss,rs,ls,
                            credit.at[j.part],give=j.chunk+RING<nchunk-1,take=j.chunk>=RING))
    pid=pl.program_id(0)
    def col(ref,f): return ref.at[:,pl.ds(f*d,d)]
    names={"g":g,"du":du,"dm":dm,"c":c,"at":at_h,"db":db,"a":a,"w":w}
    plan_l=[]
    for f in range(nf): plan_l.append((("g",f),0 if f%2==0 else 2,1,True))
    for f in range(nf): plan_l.append((("du",f),0 if (nf+f)%2==0 else 2,3,False))
    load={i:[] for i in range(-1,2*nf+2)}
    load[-1]+= [(("dm",0),1),(("c",0),3)]
    for i,(what,s,other,_) in enumerate(plan_l):
        load[max(i-2,-1)].append((what,s))
    n0=2*nf+1
    s_at=0 if (2*nf)%2==0 else 2
    load[2*nf-2].append((("at",0),s_at))
    load[nf].append((("db",0),1))
    load[2*nf-1].append((("a",0),3))
    load[2*nf]+= [(("w",0),0),(("w",1),1),(("w",2),2)]
    def copy_of(what,s):
        name,f=what
        if name=="w": return pltpu.make_async_copy(col(w,f),pool.at[s,pl.ds(0,d),:],pool_sem.at[s])
        if name in ("g","du"): return pltpu.make_async_copy(col(names[name],f),pool.at[s],pool_sem.at[s])
        return pltpu.make_async_copy(names[name],pool.at[s],pool_sem.at[s])
    waiting={}
    def fetch_after(i):
        for what,s in load.get(i,[]):
            copy_of(what,s).start(); waiting[s]=what
    def ready(s):
        if s in waiting: copy_of(waiting.pop(s),s).wait()
    scale=wt[0]
    steps=[]
    for i,(what,s,other,first) in enumerate(plan_l): steps.append(("w",i,s,other) if first else ("w",i,other,s))
    steps.append(("w",2*nf,s_at,1))
    for h in range(nhead*nblk): steps.append(("h",h))
    for n in range(3): steps.append(("x",n))
    for r in range(nrow): steps.append(("r",r))
    n_h=n0; n_x=n0+nhead*nblk; n_r=n_x+3; n_end=n_r+nrow

    def weight_step(chunk,lhs,rhs):
        if chunk>=RING:
            for p in range(2): runs[2*(chunk-RING)+p].sent()
        if chunk in shares:
            for p in range(2): runs[2*shares[chunk]+p].close()
        stage[chunk%RING]=scale*mm(lhs,rhs,0,0)
        for p in range(2): runs[2*chunk+p].start(0)

    def before(i):
        for it in segments[i]: runs[it[1]].finish(it[2])
    segments=[[]]
    for it in items:
        if it[0]=="step": segments.append([])
        else: segments[-1].append(it)
    for i,st in enumerate(steps+[("end",)]):
        kind=st[0]
        need = segments[i] or kind in ("w","x","end") or i==0 or i==n_r
        if not need: continue
        @pl.when(pid==i)
        def _(i=i,st=st,kind=kind):
            if i==0:
                sem=pltpu.get_barrier_semaphore()
                for bit in bits:
                    pl.semaphore_signal(sem,inc=1,device_id=partner(bit),device_id_type=MESH)
                pl.semaphore_wait(sem,len(bits))
                fetch_after(-1)
                small[...]=jnp.zeros_like(small)
                small[3:3+nf+2,:]=scale*mid[0:nf+2,:]
                small[nf+6:nf+7,:]=scale*mid[nf+2:nf+3,:]
                small[nf+8:nf+9,:]=scale*mid[nf+3:nf+4,:]
            before(i)
            if kind=="w":
                _,n,ls_,rs_=st
                ready(ls_); ready(rs_)
                weight_step(n,pool[ls_],pool[rs_])
                fetch_after(n)
            elif kind=="x":
                n=st[1]
                if n==0:
                    for s in range(4): ready(s)
                weight_step(n0+n,pool[3],dqkv[:,n*d:(n+1)*d])
            elif kind=="end":
                for r in runs: r.close()
    @pl.when((pid>=n_h)&(pid<n_x))
    def _():
        ib=lax.rem(pid-n_h,nblk); hp=(pid-n_h)//nblk
        rows=pl.ds(pl.multiple_of(ib*ob,ob),ob)
        lanes=pl.ds(pl.multiple_of(hp*2*HD,2*HD),2*HD)
        @pl.when(ib==0)
        def _():
            kt_s[...]=k[...].T
            dk_s[...]=jnp.zeros_like(dk_s); dv_s[...]=jnp.zeros_like(dv_s)
        lane=lax.broadcasted_iota(jnp.int32,(1,2*HD),1)//HD
        half=lax.broadcasted_iota(jnp.int32,(8,2*HD),1)//HD
        pick=jnp.where(half==lax.broadcasted_iota(jnp.int32,(8,2*HD),0),1.0,0.0).astype(BF)
        same=sc[...]==sr[:,rows]
        dd=do[rows,:].astype(F32)*at[rows,:].astype(F32)
        hi=dd.astype(BF); rest=dd-hi.astype(F32); mid_=rest.astype(BF); low=(rest-mid_.astype(F32)).astype(BF)
        delta=mm(pick,hi,1,1)+(mm(pick,mid_,1,1)+mm(pick,low,1,1))
        dqs=[]
        for h in range(2):
            qm=jnp.where(lane==h,q[rows,:],0)
            dom=jnp.where(lane==h,do[rows,:],0)
            s=mm(k[...],qm,1,1)
            p=jnp.where(same,jnp.exp(s-lse[0,h:h+1,rows]),0.0)
            dp=mm(v[...],dom,1,1)
            ds=(p*(dp-delta[h:h+1,:])).astype(BF)
            dv_s[...]+=mm(p.astype(BF),dom)
            dk_s[...]+=mm(ds,qm)
            dqs.append(mm(kt_s[h*HD:(h+1)*HD,:],ds))
        dq_s[rows,:]=jnp.concatenate(dqs,axis=0).T*(1.0/math.sqrt(HD))
        @pl.when(ib==nblk-1)
        def _():
            m=avg_matrix()[:2*HD,:2*HD]
            def avg(y):
                yh=y.astype(BF)
                return mm(yh,m)+mm((y-yh.astype(F32)).astype(BF),m)
            for n,(gr,un,rr) in enumerate(((dq_s,qu,qr),(dk_s,ku,kr))):
                gg=gr[...]; u=un[...].astype(F32)
                e=gg*qg[n:n+1,:]
                back=(rr[...]*(e-avg(e)-u*avg(e*u))).astype(BF)
                dqkv[:,pl.ds(pl.multiple_of(n*d+hp*2*HD,2*HD),2*HD)]=back
                small[n:n+1,lanes]=scale*jnp.sum(back.astype(F32),axis=0,keepdims=True)
                small[nf+9+n:nf+10+n,lanes]=scale*jnp.sum(gg*u,axis=0,keepdims=True)
                small[nf+11+n:nf+12+n,lanes]=scale*jnp.sum(gg,axis=0,keepdims=True)
            back=dv_s[...].astype(BF)
            dqkv[:,pl.ds(pl.multiple_of(2*d+hp*2*HD,2*HD),2*HD)]=back
            small[2:3,lanes]=scale*jnp.sum(back.astype(F32),axis=0,keepdims=True)
    @pl.when((pid>=n_r)&(pid<n_end))
    def _():
        rb=x.shape[0]
        rows=pl.ds(pl.multiple_of((pid-n_r)*rb,rb),rb)
        da=mm(dqkv[rows,0:d],pool[0,:d,:],1,1)+mm(dqkv[rows,d:2*d],pool[1,:d,:],1,1)+mm(dqkv[rows,2*d:],pool[2,:d,:],1,1)
        unit,r=row_norm(x[...].astype(F32))
        e=da*ng[0:1,:]
        tg_o[...]=dh[...]+r*(e-jnp.mean(e,axis=-1,keepdims=True)-unit*jnp.mean(e*unit,axis=-1,keepdims=True))
        small[nf+5:nf+6,:]+=scale*jnp.sum(da*unit,axis=0,keepdims=True)
        small[nf+7:nf+8,:]+=scale*jnp.sum(da,axis=0,keepdims=True)
        @pl.when(pid==n_end-1)
        def _():
            for p in range(2): runs[2*(nchunk-1)+p].start(0)

def backward(wt,g,du,dm,c,at,db,a,w,q,k,v,do,lse,qu,ku,qr,kr,sr,sc,qg,mid,x,dh,ng,nb,nd,ob=256,rb=256):
    t,d=x.shape; ff=g.shape[1]; nf=ff//d
    nhead=d//(2*HD); nblk=t//ob; nrow=t//rb
    n0=2*nf+1
    chunks=[(0,f*d,0,d,d) for f in range(nf)]+[(1,0,f*d,d,d) for f in range(nf)]+[(2,0,0,d,d)]
    chunks+=[(3,0,n*d,d,d) for n in range(3)]+[(4,0,0,32,d)]
    nchunk=len(chunks)
    shares={n0+n:n for n in range(3)}
    jobs=make_jobs(chunks,nb,nd)
    steps=[(n,1.9) for n in range(n0)]+[(None,1.8)]*(nhead*nblk)+[(n0+n,1.9) for n in range(3)]+[(None,2.0)]*(nrow-1)+[(nchunk-1,2.0)]
    items,_=schedule(jobs,steps,RING,shares)
    bits=bits_of(nb,nd)
    n_h=n0; n_x=n0+nhead*nblk; n_r=n_x+3; n_end=n_r+nrow
    def head(i): return jnp.clip((i-n_h)//nblk,0,nhead-1)
    def row(i): return jnp.clip(i-n_r,0,nrow-1)
    any_=pl.BlockSpec(memory_space=pltpu.HBM)
    colspec=pl.BlockSpec((t,2*HD),lambda i:(0,head(i)))
    rows=pl.BlockSpec((rb,d),lambda i:(row(i),0))
    in_specs=[pl.BlockSpec(memory_space=pltpu.SMEM)]+[any_]*8+[colspec]*5+[pl.BlockSpec((1,2,t),lambda i:(head(i),0,0))]+[colspec]*4
    in_specs+=[whole(sr),whole(sc),pl.BlockSpec((2,2*HD),lambda i:(0,0)),whole(mid),rows,rows,whole(ng)]
    out_specs=[any_]*5+[rows]
    S=jax.ShapeDtypeStruct
    out_shape=[S((ff,d),F32),S((d,ff),F32),S((d,d),F32),S((d,3*d),F32),S((32,d),F32),S((t,d),F32)]
    half=(d//2)//2
    scratch=[pltpu.VMEM((4,t,d),BF),pltpu.VMEM((RING,d,d),F32),pltpu.VMEM((2*RING,half,d),F32),pltpu.VMEM((t,3*d),BF)]
    scratch+=[pltpu.VMEM((t,2*HD),F32)]*3+[pltpu.VMEM((2*HD,t),BF),pltpu.VMEM((32,d),F32),pltpu.SemaphoreType.DMA((4,)),pltpu.SemaphoreType.REGULAR((2,))]
    own=nchunk-len(shares)-1
    for n in range(own+1):
        small=n==own
        for p in range(2):
            j=jobs[2*(nchunk-1 if small else n)+p]
            scratch.append(pltpu.VMEM(j.levels[0][3],F32))
            for lv in j.levels[0 if small else 1:]: scratch.append(pltpu.VMEM(lv[3],F32))
    for j in jobs:
        L=len(j.levels)
        scratch+=[pltpu.SemaphoreType.DMA((2*L,)),pltpu.SemaphoreType.DMA((2*L,)),pltpu.SemaphoreType.DMA((1,))]
    plan=(jobs,items,nchunk,nf,nhead,nblk,nrow,shares,bits)
    return pl.pallas_call(functools.partial(back_kernel,plan),grid=(n_end+1,),in_specs=in_specs,out_specs=out_specs,out_shape=out_shape,
        scratch_shapes=scratch,
        compiler_params=pltpu.CompilerParams(collective_id=7,has_side_effects=True,vmem_limit_bytes=63<<20),name="backward")(
        wt,g,du,dm,c,at,db,a,w,q,k,v,do,at,lse,qu,ku,qr,kr,sr,sc,qg,mid,x,dh,ng)


def body(
    tokens,
    segment,
    live,
    group_patches,
    qkv_weight,
    qkv_bias,
    out_weight,
    out_bias,
    fc1_weight,
    fc1_bias,
    fc2_weight,
    fc2_bias,
    norm_gain,
    norm_shift,
    qk_gain,
    qk_shift,
    cotangent,
):
    row_count, features = tokens.shape
    heads = features // HD
    counts = group_patches.astype(jnp.float32)
    own_count = jnp.sum(
        jnp.where(jnp.arange(counts.shape[0]) == lax.axis_index("bucket"), counts, 0.0)
    )
    weighting = own_count / (jnp.sum(counts) * math.sqrt(row_count * lax.axis_size("dp")))
    wt = weighting.reshape(1)
    seg_row, seg_col = segment[None, :], segment[:, None]
    gains = jnp.tile(qk_gain, (1, heads))
    shifts = jnp.tile(qk_shift, (1, heads))
    a_low, q_low, k_low, v_low, q_unit, k_unit, q_inv, k_inv = qkv_forward(
        tokens, qkv_weight, qkv_bias[None], norm_gain, norm_shift, gains, shifts
    )
    attn_low, lse = attend_forward(q_low, k_low, v_low, seg_row, seg_col)
    out, dhid, dattn, g_low, du_low, dm_low, c_low, db_low, mid_sums = mlp(
        tokens,
        cotangent,
        live[:, None],
        attn_low,
        out_weight,
        out_bias[None],
        fc1_weight,
        fc1_bias[None],
        fc2_weight,
        fc2_bias[None],
        norm_gain,
        norm_shift,
    )
    fc2_grad, fc1_grad, out_grad, qkv_grad, small, tokens_grad = backward(
        wt, g_low, du_low, dm_low, c_low, attn_low, db_low, a_low, qkv_weight,
        q_low, k_low, v_low, dattn, lse, q_unit, k_unit, q_inv, k_inv,
        seg_row, seg_col, gains, mid_sums, tokens, dhid, norm_gain,
        lax.axis_size("bucket"), lax.axis_size("dp"),
    )
    wide = fc1_weight.shape[1] // features
    per_head = small[wide + 9 : wide + 13].reshape(4, heads, HD).sum(axis=1)
    return (
        out,
        tokens_grad,
        qkv_grad,
        small[:3].reshape(-1),
        out_grad,
        small[3],
        fc1_grad,
        small[4 : wide + 4].reshape(-1),
        fc2_grad,
        small[wide + 4],
        small[wide + 5 : wide + 7],
        small[wide + 7 : wide + 9],
        per_head[:2],
        per_head[2:],
    )


def solution(mesh):
    return jax.shard_map(
        body,
        mesh=mesh,
        in_specs=(
            P(("bucket", "dp"), None),
            P(("bucket", "dp")),
            P(("bucket", "dp")),
            *((P(),) * 13),
            P(("bucket", "dp"), None),
        ),
        out_specs=(P(("bucket", "dp"), None), P(("bucket", "dp"), None), *((P(),) * 12)),
        check_vma=False,
    )
```

time: 2010 us -> 423 us (0.21)
  waiting for transfers between devices: 1200 us -> 0 us
  Pallas kernels: 0 us -> 384 us
  matrix products: 299 us -> 0 us
  local copies, waits for them, and re-layouts: 243 us -> 38.7 us
  other arithmetic: 156 us -> 1.29 us
  blocking collectives: 77.1 us -> 0 us
    unnamed x7 -> x0, waiting for transfers between devices: 836 us -> none
    pallas_call x0 -> x4, Pallas kernels: none -> 384 us  [the longest x1 299 us: backward(): pl.pallas_call(functools.partial(back_kernel, plan), grid=(n_end + 1,), i...]
    dot_general x26 -> x0, matrix products: 299 us -> none  [the longest x1 48.4 us: body(): jnp.dot(c_low, fc1_weight, preferred_element_type=jnp.float32) + fc1_bias]
    all_gather x4 -> x0, waiting for transfers between devices: 290 us -> none  [the longest x1 130 us: body(): lax.all_gather(merged[2], 'dp', axis=0, tiled=True)]
    psum x1 -> x0, waiting for transfers between devices: 74.4 us -> none  [body(): lax.psum((weighting * shares[0], weighting * shares[1], weighting * share...]
    reshape x15 -> x3, local copies, waits for them, and re-layouts: 72.7 us -> 1.3 us  [the longest x1 0.61 us: body(): small[:3].reshape(-1)]
    reduce_sum x15 -> x1, other arithmetic: 67.1 us -> 0.02 us  [body(): per_head = small[wide + 9:wide + 13].reshape(4, heads, HD).sum(axis=1)]
    dynamic_update_slice x4 -> x0, local copies, waits for them, and re-layouts: 65.9 us -> none  [body(): lax.map(forward_block, jnp.arange(block_count, dtype=jnp.int32))]
  transfers between devices with their start and end apart: 6 -> 0, of which waited for: 5 -> 0; matrix products, arithmetic and copies ran while one was open for 4% -> 0% of each run, Pallas kernels for 0% -> 0%
where the time goes in v2:
time: 423 us; the launch traced here: 426 us
  Pallas kernels  384 us (91%)
  local copies, waits for them, and re-layouts  38.7 us (9%)
    pallas_call x1, Pallas kernels, backward(): pl.pallas_call(functools.partial(back_kernel, plan), grid=(n_end + 1,), i...  299 us
    pallas_call x1, Pallas kernels, attend_forward(): pl.pallas_call(attend_kernel, grid=(hp,), in_specs=[col, col, col, whole(...  37.1 us
    pallas_call x1, Pallas kernels, mlp(): pl.pallas_call(functools.partial(mlp_kernel, nf), grid=(t // rb,), in_spe...  35.4 us
    unnamed x19, local copies, waits for them, and re-layouts  22.5 us
    pallas_call x1, Pallas kernels, qkv_forward(): pl.pallas_call(qkv_kernel, grid=(t // rb,), in_specs=[rows, whole(w), who...  12.5 us

profile of v2, /device:TPU:0, one launch (start us, length us, event | category | flops | bytes accessed | tf_op | source)
XLA Modules:
  0.0 425.7 jit_solution(3225558782713450210)
XLA Ops:
  0.6 1.3 convert_reduce_fusion
  3.2 1.3 broadcast_in_dim.29.bo
  4.5 1.3 broadcast_in_dim.31.b2
  5.8 1.3 broadcast_in_dim.26.b
  7.1 0.7 tile.8
  7.7 0.7 tile.9.qg.refs_21_
  8.4 0.7 tile.20
  9.1 0.7 tile.21.qs
  9.8 1.7 copy.31.sc.refs_20_
  11.5 1.7 copy.32.live
  13.2 12.5 %norm_qkv.1 = (bf16[1024,768]{1,0:T(8,128)(2,1)}, bf16[1024,768]{1,0:T(8,128)(2,1)}, bf16[1024,768]{1,0:T(8,128)(2,1)}, bf16[1024,768]{1,0:T(8,128)(2,1)}, bf16[...) custom-call(bf16[1024,768]{1,0:T(8,128)(2,1)} %refs_23_.1, ...), custom_call_target="tpu_custom_call" | custom-call | tf_op jit(solution)/shard_map/norm_qkv/pallas_call | solution.py:67
  25.7 37.1 %attend.1 = (bf16[1024,768]{1,0:T(8,128)(2,1)}, f32[6,2,1024]{2,1,0:T(2,128)}) custom-call(bf16[1024,768]{1,0:T(8,128)(2,1)} %get-tuple-element.39.q.refs_9_, bf16[1024,768]{1,0:T(8,128)(2,1)} %get-tuple-element.40.k.refs_10_, bf16[1024,768]{1,0:T(8,128)(2,1)} %get-tuple-element.41.v.refs_11_, s32[1,1024]{1,0:T(1,128)} %bitcast.10, s32[1024,1]{1,0:T(8,128)} %copy.31.sc.refs_20_), custom_call_target="tpu_custom_call" | custom-call | tf_op jit(solution)/shard_map/attend/pallas_call | solution.py:96
  62.9 35.4 %mlp.1 = (bf16[1024,768]{1,0:T(8,128)(2,1)}, f32[1024,768]{1,0:T(8,128)}, bf16[1024,768]{1,0:T(8,128)(2,1)}, bf16[1024,3072]{1,0:T(8,128)(2,1)}, bf16[1024,3072]...) custom-call(bf16[1024,768]{1,0:T(8,128)(2,1)} %refs_23_.1, ...), custom_call_target="tpu_custom_call" | custom-call | tf_op jit(solution)/shard_map/mlp/pallas_call | solution.py:149
  98.2 298.5 %backward.1 = (f32[3072,768]{1,0:T(8,128)}, f32[768,3072]{1,0:T(8,128)}, f32[768,768]{1,0:T(8,128)}, f32[768,2304]{1,0:T(8,128)}, f32[32,768]{1,0:T(8,128)}, /*index=5*/f32[1024,768]{1,0:T(8,128)}) custom-call(f32[1]{0:T(128)} %bitcast.4.refs_0_, bf16[1024,3072]{1,0:T(8,128)(2,1)} %get-tuple-element.44.refs_1_, ...), custom_call_target="tpu_custom_call" | custom-call | tf_op jit(solution)/shard_map/backward/pallas_call | solution.py:540
  396.7 1.4 slice_reduce_fusion
  398.1 0.7 slice.27
  399.5 1.4 fusion.2
  400.9 0.8 fusion.1
  403.0 3.9 copy.39
  406.9 6.8 %copy.40 = f32[768,2304]{1,0:T(8,128)} copy(f32[768,2304]{1,0:T(8,128)} %get-tuple-element.90) | data formatting | bytes 14155776
  413.7 1.4 copy.41
  415.1 4.8 %copy.42 = f32[768,3072]{1,0:T(8,128)} copy(f32[768,3072]{1,0:T(8,128)S(1)} %bitcast.8) | data formatting | bytes 18874368
  419.9 1.6 slice-done.1
  421.7 3.7 copy.43
  (20 shorter events, 2.1 us)
Async XLA Ops:
  403.0 12.1 %slice-start.3 = ((s8[9437184]{0:T(1024)(128)(4,1)}), s8[4194304]{0:T(1024)(128)(4,1)S(1)}, s32[]{:S(2)}) async-start(s8[9437184]{0:T(1024)(128)(4,1)} %bitcast.7), calls=%async_computation.3 | async-start | bytes 8388608
  406.9 6.8 %copy-start = (f32[768,768]{1,0:T(8,128)S(1)}, f32[768,768]{1,0:T(8,128)}, u32[]{:S(2)}) copy-start(f32[768,768]{1,0:T(8,128)} %get-tuple-element.92) | copy-start | bytes 7077892
  406.9 8.2 %slice-start.4 = ((s8[9437184]{0:T(1024)(128)(4,1)}), s8[4194304]{0:T(1024)(128)(4,1)S(1)}, s32[]{:S(2)}) async-start(s8[9437184]{0:T(1024)(128)(4,1)} %bitcast.7), calls=%async_computation.4 | async-start | bytes 8388608
  406.9 8.2 %slice-start.5 = ((s8[9437184]{0:T(1024)(128)(4,1)}), s8[1048576]{0:T(1024)(128)(4,1)S(1)}, s32[]{:S(2)}) async-start(s8[9437184]{0:T(1024)(128)(4,1)} %bitcast.7), calls=%async_computation.5 | async-start | bytes 2097152
  413.7 6.2 %slice-start = ((s8[9437184]{0:T(1024)(128)(4,1)}), s8[4194304]{0:T(1024)(128)(4,1)S(1)}, s32[]{:S(2)}) async-start(s8[9437184]{0:T(1024)(128)(4,1)} %bitcast.5), calls=%async_computation | async-start | bytes 8388608
  415.1 6.4 %slice-start.1 = ((s8[9437184]{0:T(1024)(128)(4,1)}), s8[4194304]{0:T(1024)(128)(4,1)S(1)}, s32[]{:S(2)}) async-start(s8[9437184]{0:T(1024)(128)(4,1)} %bitcast.5), calls=%async_computation.1 | async-start | bytes 8388608
  415.1 6.6 %slice-start.2 = ((s8[9437184]{0:T(1024)(128)(4,1)}), s8[1048576]{0:T(1024)(128)(4,1)S(1)}, s32[]{:S(2)}) async-start(s8[9437184]{0:T(1024)(128)(4,1)} %bitcast.5), calls=%async_computation.2 | async-start | bytes 2097152
